TPU v7x, 256 devices: a whole 4x4x8 slice. The times are simulated.
256 devices in a mesh: tm: 64 (over x, z, core), mp: 4 (over y).
Axes of the slice: x: 4, y: 4, z: 8, core: 2. Of those that a mesh axis runs over, the one named last changes fastest.
Arguments:
- features: bfloat16 [2048, 2048], P('tm'), may hold values from -6 to 6
- w_in: bfloat16 [2048, 4096], P(None, 'mp'), may hold values from -0.125 to 0.125
- b_in: float32 [4096], P('mp'), may hold values from -5 to 5
- output_weight: bfloat16 [4096, 256], P('mp'), may hold values from -0.09375 to 0.09375
- final_offset_entries: float32 [256], replicated, may hold values from -3 to 3
- transition: float32 [256, 256], replicated, may hold values from -1 to 1
- gains: float32 [2048, 256], P('tm'), may hold values from 0 to 1
- smooth_gains: float32 [2048, 256], P('tm'), may hold values from 0 to 1
Outputs:
- filtered: float32 [2048, 256], P(('tm', 'mp'))
- smoothed: float32 [2048, 256], P(('tm', 'mp'))
All inputs are finite; a program needn't handle non-finite values.
Results may differ from a plain program's by a relative error of at most 0.0021.
Values sent between devices are 32-bit elements; how exact they have to be, the bound alone decides.
No kernel may reach another device: no remote copies, remote signals or barrier semaphores. Data moves between devices by JAX's collectives and lax.ppermute only.
A program may use at most 128 MiB of HBM per device.

v0:
```python
import jax
import jax.numpy as jnp
from jax import lax
from jax.experimental import pallas as pl
from jax.experimental.pallas import tpu as pltpu
from jax.sharding import Mesh
from jax.sharding import PartitionSpec as P

TM = ("x", "z", "c")
F32, BF16 = jnp.float32, jnp.bfloat16
SUB = 8
VEC = 8


def pieces(a):
    high = a.astype(BF16)
    return high, (a - high.astype(F32)).astype(BF16)


def left(a):
    high, low = pieces(a)
    return jnp.concatenate([high, low, high], axis=1)


def right(b):
    high, low = pieces(b)
    return jnp.concatenate([high, high, low], axis=0)


def times(a, b3):
    return jnp.dot(left(a), b3, preferred_element_type=F32)


def each(ref, t, chains):
    return jnp.concatenate([ref[SUB * j + t : SUB * j + t + 1, :] for j in range(chains)], axis=0)


def block_kernel(gains_ref, transition_ref, chain_ref, prefix_ref):
    grid = transition_ref.shape[0]
    chains = chain_ref.shape[0]
    flipped = transition_ref[...].T
    step = right(flipped)
    for j in range(chains):
        chain_ref[j] = flipped * (1.0 - gains_ref[SUB * j : SUB * j + 1, :])
    for t in range(1, SUB):
        for part in range(2):
            own = range(part * chains // 2, (part + 1) * chains // 2)
            moved = times(jnp.concatenate([chain_ref[j] for j in own], axis=0), step)
            for n, j in enumerate(own):
                row = SUB * j + t
                keep = 1.0 - gains_ref[row : row + 1, :]
                chain_ref[j] = moved[n * grid : (n + 1) * grid] * keep
    prefix_ref[0] = chain_ref[0]
    for j in range(1, chains):
        prefix_ref[j] = times(prefix_ref[j - 1], right(chain_ref[j]))


def response_kernel(
    partial_ref, offset_ref, gains_ref, transition_ref, chain_ref, prefix_ref,
    whole_ref, drive_ref, start_ref,
):
    chains, grid = chain_ref.shape[0], transition_ref.shape[0]
    step = right(transition_ref[...].T)
    measured = partial_ref[0] + partial_ref[1] + partial_ref[2] + partial_ref[3]
    drive_ref[...] = gains_ref[...] * (measured + offset_ref[...])
    state = each(drive_ref, 0, chains)
    for t in range(1, SUB):
        keep = 1.0 - each(gains_ref, t, chains)
        state = times(state, step) * keep + each(drive_ref, t, chains)
    start_ref[...] = jnp.zeros_like(start_ref)
    carried = state[0:1]
    for j in range(1, chains):
        start_ref[j : j + 1, :] = carried
        carried = times(carried, right(chain_ref[j])) + state[j : j + 1]
    whole_ref[0:grid, :] = prefix_ref[chains - 1]
    whole_ref[grid:, :] = jnp.concatenate([carried, jnp.zeros((VEC - 1, grid), F32)], axis=0)


def after(earlier, later):
    grid = later.shape[1]
    added = jnp.concatenate([jnp.zeros((grid, grid), F32), later[grid:]], axis=0)
    return times(earlier, right(later[:grid])) + added


def pair_kernel(both_ref, whole_ref):
    whole_ref[...] = after(both_ref[0], both_ref[1])


def quad_kernel(place_ref, own_ref, others_ref, whole_ref, before_ref, held):
    grid = own_ref.shape[1]
    half = grid // 2
    place = place_ref[0]
    held[0] = own_ref[...]
    for s in range(1, 4):
        held[s, 0:half, :] = others_ref[0, s - 1, 0:half, :]
        held[s, half:grid, :] = others_ref[1, s - 1, 0:half, :]
        held[s, grid:, :] = others_ref[0, s - 1, half:, :]
    before_ref[...] = jnp.zeros_like(before_ref)
    total = held[lax.rem(place, 4)]
    for i in range(1, 4):
        @pl.when(place == i)
        def _(total=total):
            before_ref[...] = total
        total = after(total, held[lax.rem(place - i + 4, 4)])
    whole_ref[...] = total


def advance(state, whole):
    grid = whole.shape[1]
    return times(state, right(whole[:grid])) + whole[grid : grid + 1]


def hop_kernel(state_ref, whole_ref, out_ref):
    out_ref[...] = advance(state_ref[...], whole_ref[...])


def final_kernel(
    place_ref, state_ref, quad_ref, pair_ref, core_ref, prefix_ref, start_ref, drive_ref,
    gains_ref, smooth_ref, transition_ref,
    filtered_ref, weight_ref, value_ref, send_ref, found, scan_d, scan_v,
):
    chains = prefix_ref.shape[0]
    frames, grid = drive_ref.shape
    quad, pair, core, part, last = (place_ref[k] for k in range(5))
    step = right(transition_ref[...].T)
    state = state_ref[...]
    state = jnp.where(quad > 0, advance(state, quad_ref[...]), state)
    state = jnp.where(pair > 0, advance(state, pair_ref[0]), state)
    state = jnp.where(core > 0, advance(state, core_ref[0]), state)
    rows = [state[0:1]]
    for j in range(1, chains):
        rows.append(times(state, right(prefix_ref[j - 1]))[0:1] + start_ref[j : j + 1, :])
    now = jnp.concatenate(rows, axis=0)
    for t in range(SUB):
        keep = 1.0 - each(gains_ref, t, chains)
        now = times(now, step) * keep + each(drive_ref, t, chains)
        for j in range(chains):
            found[SUB * j + t : SUB * j + t + 1, :] = now[j : j + 1]
    weight = smooth_ref[...]
    row = lax.broadcasted_iota(jnp.int32, (frames, grid), 0)
    weight = jnp.where((row == frames - 1) & (last > 0), 0.0, weight)
    value = found[...] - weight * times(found[...], step)
    d, v = weight[frames - 1 : frames], value[frames - 1 : frames]
    scan_d[frames - 1 : frames, :] = d
    scan_v[frames - 1 : frames, :] = v
    for t in range(frames - 2, -1, -1):
        v = weight[t : t + 1] * v + value[t : t + 1]
        d = weight[t : t + 1] * d
        scan_d[t : t + 1, :] = d
        scan_v[t : t + 1, :] = v
    share = filtered_ref.shape[0]
    mine = pl.ds(pl.multiple_of(part * share, share), share)
    filtered_ref[...] = found[mine, :]
    weight_ref[...] = scan_d[mine, :]
    value_ref[...] = scan_v[mine, :]
    send_ref[...] = jnp.broadcast_to(jnp.concatenate([d, v], axis=1), send_ref.shape)


def smooth_kernel(place_ref, got_ref, weight_ref, value_ref, smoothed_ref):
    blocks = got_ref.shape[0]
    grid = weight_ref.shape[1]
    here = place_ref[5]
    row = lax.broadcasted_iota(jnp.int32, (blocks, grid), 0)
    d = jnp.where(row > here, got_ref[:, :grid], 1.0)
    v = jnp.where(row > here, got_ref[:, grid:], 0.0)
    later = jnp.zeros((1, grid), F32)
    for k in range(blocks - 1, -1, -1):
        later = d[k : k + 1] * later + v[k : k + 1]
    smoothed_ref[...] = weight_ref[...] * later + value_ref[...]


def shape(*dims):
    return jax.ShapeDtypeStruct(dims, F32)


V = pl.BlockSpec(memory_space=pltpu.VMEM)
S = pl.BlockSpec(memory_space=pltpu.SMEM)
ROOM = pltpu.CompilerParams(vmem_limit_bytes=48 << 20)


def call(kernel, ins, outs, out_shape, scratch=()):
    return pl.pallas_call(
        kernel, in_specs=ins, out_specs=outs, out_shape=out_shape,
        scratch_shapes=list(scratch), compiler_params=ROOM,
    )


def on_device(
    features, w_in, b_in, output_weight, final_offset_entries, transition, gains, smooth_gains
):
    frames, grid = gains.shape
    chains = frames // SUB
    rows = grid + VEC
    x, z, c, part = (lax.axis_index(a) for a in ("x", "z", "c", "y"))
    blocks = lax.axis_size(TM)
    here = lax.axis_index(TM)
    quad = z // 2
    last = (here == blocks - 1).astype(jnp.int32)
    place = jnp.stack([quad, z % 2, c, part, last, here]).astype(jnp.int32)

    pre = jnp.dot(features, w_in, preferred_element_type=F32) + b_in
    hidden = jax.nn.gelu(pre, approximate=True).astype(BF16)
    partial = jnp.dot(hidden, output_weight, preferred_element_type=F32)
    parts = lax.axis_size("y")
    partials = lax.all_to_all(
        jnp.broadcast_to(partial, (parts, frames, grid)), "y", 0, 0, tiled=True
    )

    chain, prefix = call(
        block_kernel, [V, V], [V, V],
        [shape(chains, grid, grid), shape(chains, grid, grid)],
    )(gains, transition)
    whole, drive, start = call(
        response_kernel, [V] * 6, [V] * 3,
        [shape(rows, grid), shape(frames, grid), shape(VEC, grid)],
    )(partials, final_offset_entries[None], gains, transition, chain, prefix)

    cores = lax.all_gather(whole, "c")
    pair = call(pair_kernel, [V], V, shape(rows, grid))(cores)
    pairs = lax.all_gather(
        pair, "z", axis_index_groups=[[2 * k, 2 * k + 1] for k in range(4)]
    )
    four = call(pair_kernel, [V], V, shape(rows, grid))(pairs)
    half = grid // 2
    mine = jnp.concatenate(
        [lax.dynamic_slice_in_dim(four, c * half, half, 0), four[grid:]], axis=0
    )
    others = jnp.stack(
        [
            lax.ppermute(mine, "z", [(k, (k + 2 * s) % 8) for k in range(8)])
            for s in range(1, 4)
        ]
    )
    others = lax.all_gather(others, "c")
    group, before = call(
        quad_kernel, [S, V, V], [V, V], [shape(rows, grid), shape(rows, grid)],
        [pltpu.VMEM((4, rows, grid), F32)],
    )(place, four, others)

    forward = [(k, k + 1) for k in range(3)]
    state = lax.ppermute(group[grid:], "x", forward)
    for _ in range(2):
        state = call(hop_kernel, [V, V], V, shape(VEC, grid))(state, group)
        state = lax.ppermute(state, "x", forward)

    share = frames // parts
    filtered, weight, value, send = call(
        final_kernel, [S] + [V] * 10, [V] * 4,
        [shape(share, grid)] * 3 + [shape(blocks, 2 * grid)],
        [pltpu.VMEM((frames, grid), F32)] * 3,
    )(place, state, before, pairs, cores, prefix, start, drive, gains, smooth_gains, transition)
    got = lax.all_to_all(send, TM, 0, 0, tiled=True)
    smoothed = call(smooth_kernel, [S, V, V, V], V, shape(share, grid))(
        place, got, weight, value
    )
    return filtered, smoothed


def solution(mesh):
    torus = Mesh(mesh.devices.reshape(4, 8, 2, mesh.shape["mp"]), ("x", "z", "c", "y"))
    return jax.shard_map(
        on_device,
        mesh=torus,
        in_specs=(
            P(TM, None), P(None, "y"), P("y"), P("y", None), P(), P(), P(TM, None), P(TM, None),
        ),
        out_specs=(P((*TM, "y"), None), P((*TM, "y"), None)),
        check_vma=False,
    )
```

profile of v0, /device:TPU:1, one launch (start us, length us, event | category | flops | bytes accessed | tf_op | source)
XLA Modules:
  0.0 99.6 jit_solution(13411154099962881122)
XLA Ops:
  0.6 0.0 copy-start
  0.6 0.0 copy-start.2
  0.7 0.0 copy-start.1
  0.7 0.0 copy-start.4
  0.7 1.0 %copy-done = bf16[1024,256]{1,0:T(8,128)(2,1)S(1)} copy-done((bf16[1024,256]{1,0:T(8,128)(2,1)S(1)}, bf16[1024,256]{1,0:T(8,128)(2,1)}, u32[]{:S(2)}) %copy-start) | copy-done | bytes 524312
  1.7 3.2 %fusion.8 = f32[32,256]{1,0:T(8,128)S(1)} fusion(bf16[1024,256]{1,0:T(8,128)(2,1)S(1)} %copy-done, bf16[32,2048]{1,0:T(8,128)(2,1)} %param.8, bf16[2048,1024]{1,0:T(8,128)(2,1)} %param.9, f32[1024]{0:T(1024)} %param.10), kind=kOutput, calls=%fused_computation.12 | convolution fusion | flops 151322624 | bytes 4886528 | tf_op jit(solution)/shard_map/dot_general | solution.py:203
  4.9 0.7 broadcast_in_dim.7
  5.6 5.0 %all-to-all-start = ((f32[4,32,256]{2,1,0:T(8,128)}), f32[4,32,256]{2,1,0:T(8,128)S(1)}, u32[]{:S(2)}, u32[]{:S(2)}) async-start(f32[4,32,256]{2,1,0:T(8,128)} %broadcast_in_dim.7), calls=%async_computation | async-start | bytes 262144 | tf_op jit(solution)/shard_map/all_to_all | solution.py:205
  10.6 0.0 copy-done.2
  10.6 0.0 copy-done.1
  10.6 3.9 %shard_map.95 = (f32[4,256,256]{2,1,0:T(8,128)S(1)}, f32[4,256,256]{2,1,0:T(8,128)S(1)}) custom-call(f32[32,256]{1,0:T(8,128)S(1)} %copy-done.2, f32[256,256]{1,0:T(8,128)S(1)} %copy-done.1), custom_call_target="tpu_custom_call" | custom-call | tf_op jit(solution)/shard_map/pallas_call | solution.py:209
  14.5 0.9 all-to-all-done.partial_ref
  15.4 0.0 copy-done.4
  15.4 2.0 %shard_map.96 = (f32[264,256]{1,0:T(8,128)S(1)}, f32[32,256]{1,0:T(8,128)S(1)}, f32[8,256]{1,0:T(8,128)S(1)}) custom-call(f32[4,32,256]{2,1,0:T(8,128)S(1)} %all-to-all-done.partial_ref, f32[1,256]{1,0:T(1,128)S(1)} %bitcast.27, f32[32,256]{1,0:T(8,128)S(1)} %copy-done.2, f32[256,256]{1,0:T(8,128)S(1)} %copy-done.1, ...), custom_call_target="tpu_custom_call" | custom-call | tf_op jit(solution)/shard_map/pallas_call | solution.py:213
  17.4 0.0 copy-start.3
  17.4 4.6 %all-gather = f32[528,256]{1,0:T(8,128)S(1)} all-gather(f32[264,256]{1,0:T(8,128)S(1)} %get-tuple-element.15), channel_id=2, replica_groups=mesh['x'=4,'z'=8,'c'=2,'y'=4] {'c'}, dimensions={0}, use_global_device_ids=true | all-gather | bytes 811008 | tf_op jit(solution)/shard_map/all_gather | solution.py:218
  22.0 0.3 shard_map.97
  22.3 8.4 %all-gather.1 = f32[528,256]{1,0:T(8,128)S(1)} all-gather(f32[264,256]{1,0:T(8,128)S(1)} %shard_map.97), channel_id=3, replica_groups={{0,8},{16,24},{32,40},{48,56},{1,9},{17,25},{33,41},{49,57},{2,10},{18,..., dimensions={0}, use_global_device_ids=true | all-gather | bytes 811008 | tf_op jit(solution)/shard_map/all_gather | solution.py:220
  30.7 0.3 shard_map.98.own_ref
  31.0 0.7 pad_maximum_fusion.1
  31.6 5.5 %collective-permute-start.2 = (f32[136,256]{1,0:T(8,128)}, f32[136,256]{1,0:T(8,128)S(1)}, u32[]{:S(2)}, u32[]{:S(2)}) collective-permute-start(f32[136,256]{1,0:T(8,128)} %pad_maximum_fusion.1), channel_id=1, source_target_pairs={{0,48},{8,56},{16,0},{24,8},{32,16},{40,24},{48,32},{56,40},{1,49}... | collective-permute-start | bytes 417800 | tf_op jit(solution)/shard_map/ppermute | solution.py:230
  37.1 0.9 collective-permute-start.1
  38.0 2.4 %collective-permute-start = (f32[136,256]{1,0:T(8,128)}, f32[136,256]{1,0:T(8,128)}, u32[]{:S(2)}, u32[]{:S(2)}) collective-permute-start(f32[136,256]{1,0:T(8,128)} %pad_maximum_fusion.1), channel_id=1, source_target_pairs={{0,16},{8,24},{16,32},{24,40},{32,48},{40,56},{48,0},{56,8},{1,17}... | collective-permute-start | bytes 417800 | tf_op jit(solution)/shard_map/ppermute | solution.py:230
  40.3 0.1 stack.43.place_ref
  40.4 0.0 collective-permute-done.2
  40.4 7.8 %collective-permute-done.1 = f32[136,256]{1,0:T(8,128)} collective-permute-done((f32[136,256]{1,0:T(8,128)}, f32[136,256]{1,0:T(8,128)}, u32[]{:S(2)}, u32[]{:S(2)}) %collective-permute-start.1) | collective-permute-done | bytes 139296 | tf_op jit(solution)/shard_map/ppermute | solution.py:230
  48.2 0.4 collective-permute-done
  48.6 1.0 %pad_maximum_fusion = f32[3,136,256]{2,1,0:T(8,128)S(1)} fusion(f32[1,136,256]{2,1,0:T(8,128)S(1)} %bitcast.28, f32[1,136,256]{2,1,0:T(8,128)} %bitcast.10, f32[1,136,256]{2,1,0:T(8,128)} %bitcast.9), kind=kLoop, calls=%fused_computation.1 | loop fusion | flops 208896 | bytes 835584 | tf_op jit(solution)/shard_map/stack | solution.py:228
  49.7 4.7 %all-gather.2 = f32[6,136,256]{2,1,0:T(8,128)S(1)} all-gather(f32[3,136,256]{2,1,0:T(8,128)S(1)} %pad_maximum_fusion), channel_id=4, replica_groups=mesh['x'=4,'z'=8,'c'=2,'y'=4] {'c'}, dimensions={0}, use_global_device_ids=true | all-gather | bytes 1253376 | tf_op jit(solution)/shard_map/all_gather | solution.py:234
  54.4 1.7 %shard_map.99 = (f32[264,256]{1,0:T(8,128)S(1)}, f32[264,256]{1,0:T(8,128)S(1)}) custom-call(s32[6]{0:T(128)S(1)} %stack.43.place_ref, f32[264,256]{1,0:T(8,128)S(1)} %shard_map.98.own_ref, f32[2,3,136,256]{3,2,1,0:T(8,128)S(1)} %bitcast.24), custom_call_target="tpu_custom_call" | custom-call | tf_op jit(solution)/shard_map/pallas_call | solution.py:235
  56.0 3.1 %collective-permute-start.3 = (f32[8,256]{1,0:T(8,128)S(1)}, f32[8,256]{1,0:T(8,128)S(1)}, u32[]{:S(2)}, u32[]{:S(2)}) collective-permute-start(f32[8,256]{1,0:T(8,128)S(1)} %slice.7), channel_id=1, source_target_pairs={{0,64},{64,128},{128,192},{1,65},{65,129},{129,193},{2,66},{66,130... | collective-permute-start | bytes 24584 | tf_op jit(solution)/shard_map/ppermute | solution.py:241
  59.2 0.8 collective-permute-done.3.state_ref
  59.9 0.2 shard_map.100
  60.1 3.6 %collective-permute-start.4 = (f32[8,256]{1,0:T(8,128)S(1)}, f32[8,256]{1,0:T(8,128)S(1)}, u32[]{:S(2)}, u32[]{:S(2)}) collective-permute-start(f32[8,256]{1,0:T(8,128)S(1)} %shard_map.100), channel_id=1, source_target_pairs={{0,64},{64,128},{128,192},{1,65},{65,129},{129,193},{2,66},{66,130... | collective-permute-start | bytes 24584 | tf_op jit(solution)/shard_map/ppermute | solution.py:244
  63.7 0.8 collective-permute-done.4.state_ref
  64.5 0.2 shard_map.101
  64.7 3.6 %collective-permute-start.5 = (f32[8,256]{1,0:T(8,128)S(1)}, f32[8,256]{1,0:T(8,128)S(1)}, u32[]{:S(2)}, u32[]{:S(2)}) collective-permute-start(f32[8,256]{1,0:T(8,128)S(1)} %shard_map.101), channel_id=1, source_target_pairs={{0,64},{64,128},{128,192},{1,65},{65,129},{129,193},{2,66},{66,130... | collective-permute-start | bytes 24584 | tf_op jit(solution)/shard_map/ppermute | solution.py:244
  68.3 0.8 collective-permute-done.5.state_ref
  69.1 0.0 copy-done.3
  69.1 3.5 %shard_map.102 = (f32[8,256]{1,0:T(8,128)}, f32[8,256]{1,0:T(8,128)S(1)}, f32[8,256]{1,0:T(8,128)S(1)}, f32[64,512]{1,0:T(8,128)S(1)}) custom-call(s32[6]{0:T(128)S(1)} %stack.43.place_ref, f32[8,256]{1,0:T(8,128)S(1)} %collective-permute-done.5.state_ref, f32[264,256]{1,0:T(8,128)S(1)} %get-tuple-element.17.quad_ref, f32[2,264,256]{2,1,0:T(8,128)S(1)} %bitcast.23, ...), custom_call_target="tpu_custom_call" | custom-call | tf_op jit(solution)/shard_map/pallas_call | solution.py:247
  72.6 0.1 copy.10
  72.7 25.5 %all_to_all.16 = f32[64,1,512]{2,1,0:T(1,128)S(1)} all-to-all(f32[64,1,512]{2,1,0:T(1,128)S(1)} %copy.10), channel_id=1, replica_groups=mesh['x'=4,'z'=8,'c'=2,'y'=4] {'x','z','c'}, dimensions={0} | all-to-all | bytes 262144 | tf_op jit(solution)/shard_map/all_to_all | solution.py:252
  98.2 1.3 %shard_map.103 = f32[8,256]{1,0:T(8,128)} custom-call(s32[6]{0:T(128)S(1)} %stack.43.place_ref, f32[64,512]{1,0:T(8,128)S(1)} %bitcast.25, f32[8,256]{1,0:T(8,128)S(1)} %get-tuple-element.22.weight_ref, f32[8,256]{1,0:T(8,128)S(1)} %get-tuple-element.23.value_ref), custom_call_target="tpu_custom_call" | custom-call | tf_op jit(solution)/shard_map/pallas_call | solution.py:253
  (4 shorter events, 0.0 us)
Async XLA Ops:
  0.6 1.0 %copy-start = (bf16[1024,256]{1,0:T(8,128)(2,1)S(1)}, bf16[1024,256]{1,0:T(8,128)(2,1)}, u32[]{:S(2)}) copy-start(bf16[1024,256]{1,0:T(8,128)(2,1)} %param.11) | copy-start | bytes 1572868
  0.6 9.9 %copy-start.2 = (f32[32,256]{1,0:T(8,128)S(1)}, f32[32,256]{1,0:T(8,128)}, u32[]{:S(2)}) copy-start(f32[32,256]{1,0:T(8,128)} %gains_ref.5) | copy-start | bytes 98308
  0.7 9.9 %copy-start.1 = (f32[256,256]{1,0:T(8,128)S(1)}, f32[256,256]{1,0:T(8,128)}, u32[]{:S(2)}) copy-start(f32[256,256]{1,0:T(8,128)} %transition_ref.5) | copy-start | bytes 786436
  0.7 14.7 %copy-start.4 = (f32[256]{0:T(256)S(1)}, f32[256]{0:T(256)}, u32[]{:S(2)}) copy-start(f32[256]{0:T(256)} %param.12) | copy-start | bytes 3076
  5.6 9.8 %all-to-all-start = ((f32[4,32,256]{2,1,0:T(8,128)}), f32[4,32,256]{2,1,0:T(8,128)S(1)}, u32[]{:S(2)}, u32[]{:S(2)}) async-start(f32[4,32,256]{2,1,0:T(8,128)} %broadcast_in_dim.7), calls=%async_computation | async-start | bytes 262144 | tf_op jit(solution)/shard_map/all_to_all | solution.py:205
  17.4 51.7 %copy-start.3 = (f32[32,256]{1,0:T(8,128)S(1)}, f32[32,256]{1,0:T(8,128)}, u32[]{:S(2)}) copy-start(f32[32,256]{1,0:T(8,128)} %smooth_ref.1) | copy-start | bytes 98308
  31.6 8.8 %collective-permute-start.2 = (f32[136,256]{1,0:T(8,128)}, f32[136,256]{1,0:T(8,128)S(1)}, u32[]{:S(2)}, u32[]{:S(2)}) collective-permute-start(f32[136,256]{1,0:T(8,128)} %pad_maximum_fusion.1), channel_id=1, source_target_pairs={{0,48},{8,56},{16,0},{24,8},{32,16},{40,24},{48,32},{56,40},{1,49}... | collective-permute-start | bytes 417800 | tf_op jit(solution)/shard_map/ppermute | solution.py:230
  37.1 11.1 %collective-permute-start.1 = (f32[136,256]{1,0:T(8,128)}, f32[136,256]{1,0:T(8,128)}, u32[]{:S(2)}, u32[]{:S(2)}) collective-permute-start(f32[136,256]{1,0:T(8,128)} %pad_maximum_fusion.1), channel_id=1, source_target_pairs={{0,32},{8,40},{16,48},{24,56},{32,0},{40,8},{48,16},{56,24},{1,33}... | collective-permute-start | bytes 417800 | tf_op jit(solution)/shard_map/ppermute | solution.py:230
  38.0 10.7 %collective-permute-start = (f32[136,256]{1,0:T(8,128)}, f32[136,256]{1,0:T(8,128)}, u32[]{:S(2)}, u32[]{:S(2)}) collective-permute-start(f32[136,256]{1,0:T(8,128)} %pad_maximum_fusion.1), channel_id=1, source_target_pairs={{0,16},{8,24},{16,32},{24,40},{32,48},{40,56},{48,0},{56,8},{1,17}... | collective-permute-start | bytes 417800 | tf_op jit(solution)/shard_map/ppermute | solution.py:230
  56.0 3.9 %collective-permute-start.3 = (f32[8,256]{1,0:T(8,128)S(1)}, f32[8,256]{1,0:T(8,128)S(1)}, u32[]{:S(2)}, u32[]{:S(2)}) collective-permute-start(f32[8,256]{1,0:T(8,128)S(1)} %slice.7), channel_id=1, source_target_pairs={{0,64},{64,128},{128,192},{1,65},{65,129},{129,193},{2,66},{66,130... | collective-permute-start | bytes 24584 | tf_op jit(solution)/shard_map/ppermute | solution.py:241
  60.1 4.4 %collective-permute-start.4 = (f32[8,256]{1,0:T(8,128)S(1)}, f32[8,256]{1,0:T(8,128)S(1)}, u32[]{:S(2)}, u32[]{:S(2)}) collective-permute-start(f32[8,256]{1,0:T(8,128)S(1)} %shard_map.100), channel_id=1, source_target_pairs={{0,64},{64,128},{128,192},{1,65},{65,129},{129,193},{2,66},{66,130... | collective-permute-start | bytes 24584 | tf_op jit(solution)/shard_map/ppermute | solution.py:244
  64.7 4.4 %collective-permute-start.5 = (f32[8,256]{1,0:T(8,128)S(1)}, f32[8,256]{1,0:T(8,128)S(1)}, u32[]{:S(2)}, u32[]{:S(2)}) collective-permute-start(f32[8,256]{1,0:T(8,128)S(1)} %shard_map.101), channel_id=1, source_target_pairs={{0,64},{64,128},{128,192},{1,65},{65,129},{129,193},{2,66},{66,130... | collective-permute-start | bytes 24584 | tf_op jit(solution)/shard_map/ppermute | solution.py:244
where the time goes:
time: 100 us; the launch traced here: 99.6 us
  blocking collectives  43.2 us (43%)
  starting transfers between devices  24 us (24%)
  Pallas kernels  13.2 us (13%)
  waiting for transfers between devices  11.5 us (12%)
  matrix products  3.2 us (3%)
  local copies, waits for them, and re-layouts  1.95 us (2%)
  other arithmetic  1.67 us (2%)
    all_to_all x1, blocking collectives, on_device(): got = lax.all_to_all(send, TM, 0, 0, tiled=True)  25.5 us
    ppermute x3, starting transfers between devices, on_device(): lax.ppermute(mine, 'z', [(k, (k + 2 * s) % 8) for k in range(8)])  8.7 us
    all_gather x1, blocking collectives, on_device(): lax.all_gather(pair, 'z', axis_index_groups=[[2 * k, 2 * k + 1] for k in...  8.37 us
    ppermute x3, waiting for transfers between devices, on_device(): lax.ppermute(mine, 'z', [(k, (k + 2 * s) % 8) for k in range(8)])  8.22 us
    ppermute x2, starting transfers between devices, on_device(): state = lax.ppermute(state, 'x', forward)  7.22 us
    all_to_all x1, starting transfers between devices, on_device(): lax.all_to_all(jnp.broadcast_to(partial, (parts, frames, grid)), 'y', 0,...  5.01 us
    all_gather x1, blocking collectives, on_device(): others = lax.all_gather(others, 'c')  4.71 us
    all_gather x1, blocking collectives, on_device(): cores = lax.all_gather(whole, 'c')  4.62 us
  transfers between devices with their start and end apart: 7, of which 6 were waited for; matrix products, arithmetic and copies ran while one was open for 0% of the time, Pallas kernels for 4%

commit v1 on v0

v1 whole, which is shorter than its diff:
```python
import functools

import jax
import jax.numpy as jnp
from jax import lax
from jax.experimental import pallas as pl
from jax.experimental.pallas import tpu as pltpu
from jax.sharding import Mesh
from jax.sharding import PartitionSpec as P

TM = ("x", "z", "c")
F32, BF16 = jnp.float32, jnp.bfloat16
SUB = 8
VEC = 8


def pieces(a):
    high = a.astype(BF16)
    return high, (a - high.astype(F32)).astype(BF16)


def left(a):
    high, low = pieces(a)
    return jnp.concatenate([high, low, high], axis=1)


def right(b):
    high, low = pieces(b)
    return jnp.concatenate([high, high, low], axis=0)


def times(a, b3):
    return jnp.dot(left(a), b3, preferred_element_type=F32)


def each(ref, t, chains):
    return jnp.concatenate([ref[SUB * j + t : SUB * j + t + 1, :] for j in range(chains)], axis=0)


def bit(level):
    if level == 0:
        return lax.axis_index("c")
    if level < 4:
        return (lax.axis_index("z") >> (level - 1)) & 1
    return (lax.axis_index("x") >> (level - 4)) & 1


def network_kernel(
    features_hbm, w_in_hbm, b_in_hbm, out_weight_hbm, partial_ref,
    features_ref, w_in_ref, b_in_ref, out_weight_ref, pre_ref, done,
):
    pieces_in = done.shape[0] - 3
    deep = w_in_ref.shape[0] // pieces_in
    small = [
        pltpu.make_async_copy(features_hbm, features_ref, done.at[pieces_in]),
        pltpu.make_async_copy(b_in_hbm, b_in_ref, done.at[pieces_in + 1]),
        pltpu.make_async_copy(out_weight_hbm, out_weight_ref, done.at[pieces_in + 2]),
    ]
    parts = [
        pltpu.make_async_copy(
            w_in_hbm.at[k * deep : (k + 1) * deep], w_in_ref.at[k * deep : (k + 1) * deep], done.at[k]
        )
        for k in range(pieces_in)
    ]
    for copy in (small[0], *parts, *small[1:]):
        copy.start()
    small[0].wait()
    for k, copy in enumerate(parts):
        copy.wait()
        rows = slice(k * deep, (k + 1) * deep)
        part = jnp.dot(features_ref[:, rows], w_in_ref[rows, :], preferred_element_type=F32)
        pre_ref[...] = part if k == 0 else pre_ref[...] + part
    small[1].wait()
    hidden = jax.nn.gelu(pre_ref[...] + b_in_ref[...], approximate=True).astype(BF16)
    small[2].wait()
    partial_ref[...] = jnp.dot(hidden, out_weight_ref[...], preferred_element_type=F32)


def block_kernel(gains_ref, transition_ref, chain_ref, prefix_ref):
    grid = transition_ref.shape[0]
    chains = chain_ref.shape[0]
    flipped = transition_ref[...].T
    step = right(flipped)
    for j in range(chains):
        chain_ref[j] = flipped * (1.0 - gains_ref[SUB * j : SUB * j + 1, :])
    for t in range(1, SUB):
        for part in range(2):
            own = range(part * chains // 2, (part + 1) * chains // 2)
            moved = times(jnp.concatenate([chain_ref[j] for j in own], axis=0), step)
            for n, j in enumerate(own):
                row = SUB * j + t
                keep = 1.0 - gains_ref[row : row + 1, :]
                chain_ref[j] = moved[n * grid : (n + 1) * grid] * keep
    prefix_ref[0] = chain_ref[0]
    for j in range(1, chains):
        prefix_ref[j] = times(prefix_ref[j - 1], right(chain_ref[j]))


def response_kernel(
    one_ref, two_ref, three_ref, four_ref, offset_ref, gains_ref, transition_ref, chain_ref, prefix_ref,
    whole_ref, drive_ref, start_ref,
):
    chains, grid = chain_ref.shape[0], transition_ref.shape[0]
    step = right(transition_ref[...].T)
    measured = (one_ref[...] + two_ref[...]) + (three_ref[...] + four_ref[...])
    drive_ref[...] = gains_ref[...] * (measured + offset_ref[...])
    state = each(drive_ref, 0, chains)
    for t in range(1, SUB):
        keep = 1.0 - each(gains_ref, t, chains)
        state = times(state, step) * keep + each(drive_ref, t, chains)
    start_ref[...] = jnp.zeros_like(start_ref)
    carried = state[0:1]
    for j in range(1, chains):
        start_ref[j : j + 1, :] = carried
        carried = times(carried, right(chain_ref[j])) + state[j : j + 1]
    whole_ref[0:grid, :] = prefix_ref[chains - 1]
    whole_ref[grid:, :] = jnp.concatenate([carried, jnp.zeros((VEC - 1, grid), F32)], axis=0)


def after(earlier, later):
    grid = later.shape[1]
    added = jnp.concatenate([jnp.zeros((grid, grid), F32), later[grid:]], axis=0)
    return times(earlier, right(later[:grid])) + added


def ordered(held, own, other, upper):
    held[0] = own
    held[1] = other
    return after(held[upper], held[1 - upper])


def half_rows(whole_ref, half_ref, core):
    half = half_ref.shape[0] - VEC
    half_ref[0:half, :] = whole_ref[pl.ds(pl.multiple_of(core * half, half), half), :]
    half_ref[half:, :] = whole_ref[2 * half :, :]


def whole_kernel(level, own_ref, other_ref, whole_ref, half_ref, held):
    whole_ref[...] = ordered(held, own_ref[...], other_ref[...], bit(level))
    half_rows(whole_ref, half_ref, bit(0))


def join(mine_ref, theirs_ref, other_ref):
    half = mine_ref.shape[0] - VEC
    core = bit(0)
    other_ref[pl.ds(pl.multiple_of(core * half, half), half), :] = mine_ref[0:half, :]
    other_ref[pl.ds(pl.multiple_of((1 - core) * half, half), half), :] = theirs_ref[0:half, :]
    other_ref[2 * half :, :] = mine_ref[half:, :]


def halves_kernel(level, own_ref, mine_ref, theirs_ref, whole_ref, half_ref, other_ref, held):
    join(mine_ref, theirs_ref, other_ref)
    whole_ref[...] = ordered(held, own_ref[...], other_ref[...], bit(level))
    half_rows(whole_ref, half_ref, bit(0))


def end_kernel(level, own_ref, mine_ref, theirs_ref, end_ref, other_ref, held):
    grid = own_ref.shape[1]
    upper = bit(level)
    join(mine_ref, theirs_ref, other_ref)
    held[0] = own_ref[...]
    held[1] = other_ref[...]
    later = held.at[1 - upper]
    end_ref[...] = times(held[upper, grid:, :], right(later[:grid, :])) + later[grid:, :]


def starts_kernel(*refs):
    others, (prefix_ref, start_ref, starts_ref, shifts_ref, held) = refs[:4], refs[4:]
    chains, grid = prefix_ref.shape[0], prefix_ref.shape[2]
    top = others[3]
    row = lax.broadcasted_iota(jnp.int32, top.shape, 0)
    column = lax.broadcasted_iota(jnp.int32, top.shape, 1)
    held[...] = jnp.where(bit(3) > 0, top[...], jnp.where(row == column, 1.0, 0.0))
    for level in (2, 1, 0):
        @pl.when(bit(level) > 0)
        def _():
            held[...] = after(held[...], others[level][...])
    starts_ref[0] = held[:grid, :]
    rows = [held[grid : grid + 1, :]]
    for j in range(1, chains):
        moved = times(held[...], right(prefix_ref[j - 1]))
        starts_ref[j] = moved[:grid]
        rows.append(moved[grid : grid + 1] + start_ref[j : j + 1, :])
    shifts_ref[...] = jnp.concatenate([*rows, jnp.zeros((VEC - chains, grid), F32)], axis=0)


def advance(state, whole):
    grid = whole.shape[1]
    return times(state, right(whole[:grid])) + whole[grid : grid + 1]


def final_kernel(
    end_ref, group_ref, starts_ref, shifts_ref, drive_ref, gains_ref, smooth_ref, transition_ref,
    filtered_ref, weight_ref, value_ref, send_ref, found, scan_d, scan_v,
):
    chains = starts_ref.shape[0]
    frames, grid = drive_ref.shape
    part = lax.axis_index("y")
    last = lax.axis_index(TM) == lax.axis_size(TM) - 1
    step = right(transition_ref[...].T)
    state = jnp.where(bit(5) > 0, end_ref[...], 0.0)
    state = jnp.where(bit(4) > 0, advance(state, group_ref[...]), state)
    rows = [times(state, right(starts_ref[j]))[0:1] for j in range(chains)]
    now = jnp.concatenate(rows, axis=0) + shifts_ref[0:chains, :]
    for t in range(SUB):
        keep = 1.0 - each(gains_ref, t, chains)
        now = times(now, step) * keep + each(drive_ref, t, chains)
        for j in range(chains):
            found[SUB * j + t : SUB * j + t + 1, :] = now[j : j + 1]
    weight = smooth_ref[...]
    row = lax.broadcasted_iota(jnp.int32, (frames, grid), 0)
    weight = jnp.where((row == frames - 1) & last, 0.0, weight)
    value = found[...] - weight * times(found[...], step)
    d, v = weight[frames - 1 : frames], value[frames - 1 : frames]
    scan_d[frames - 1 : frames, :] = d
    scan_v[frames - 1 : frames, :] = v
    for t in range(frames - 2, -1, -1):
        v = weight[t : t + 1] * v + value[t : t + 1]
        d = weight[t : t + 1] * d
        scan_d[t : t + 1, :] = d
        scan_v[t : t + 1, :] = v
    share = filtered_ref.shape[0]
    mine = pl.ds(pl.multiple_of(part * share, share), share)
    filtered_ref[...] = found[mine, :]
    weight_ref[...] = scan_d[mine, :]
    value_ref[...] = scan_v[mine, :]
    send_ref[...] = jnp.broadcast_to(jnp.concatenate([d, v], axis=1), send_ref.shape)


def smooth_kernel(got_ref, weight_ref, value_ref, smoothed_ref):
    blocks = got_ref.shape[0]
    grid = weight_ref.shape[1]
    here = lax.axis_index(TM)
    row = lax.broadcasted_iota(jnp.int32, (blocks, grid), 0)
    d = jnp.where(row > here, got_ref[:, :grid], 1.0)
    v = jnp.where(row > here, got_ref[:, grid:], 0.0)
    later = jnp.zeros((1, grid), F32)
    for k in range(blocks - 1, -1, -1):
        later = d[k : k + 1] * later + v[k : k + 1]
    smoothed_ref[...] = weight_ref[...] * later + value_ref[...]


def shape(*dims):
    return jax.ShapeDtypeStruct(dims, F32)


V = pl.BlockSpec(memory_space=pltpu.VMEM)
ROOM = pltpu.CompilerParams(vmem_limit_bytes=12 << 20)


def call(kernel, ins, outs, out_shape, scratch=()):
    return pl.pallas_call(
        kernel, in_specs=ins, out_specs=outs, out_shape=out_shape,
        scratch_shapes=list(scratch), compiler_params=ROOM,
    )


def on_device(
    features, w_in, b_in, output_weight, final_offset_entries, transition, gains, smooth_gains
):
    frames, grid = gains.shape
    chains = frames // SUB
    rows = grid + VEC
    blocks = lax.axis_size(TM)
    parts = lax.axis_size("y")
    H = pl.BlockSpec(memory_space=pltpu.HBM)
    units = w_in.shape[1]
    partial = call(
        network_kernel, [H] * 4, V, shape(frames, grid),
        [
            pltpu.VMEM(features.shape, BF16), pltpu.VMEM(w_in.shape, BF16),
            pltpu.VMEM((1, units), F32), pltpu.VMEM(output_weight.shape, BF16),
            pltpu.VMEM((frames, units), F32), pltpu.SemaphoreType.DMA((8 + 3,)),
        ],
    )(*(pltpu.with_memory_space_constraint(a, pltpu.HBM) for a in (features, w_in, b_in[None], output_weight)))
    partials = [partial] + [
        lax.ppermute(partial, "y", [(k, (k + s) % parts) for k in range(parts)])
        for s in range(1, parts)
    ]

    chain, prefix = call(
        block_kernel, [V, V], [V, V],
        [shape(chains, grid, grid), shape(chains, grid, grid)],
    )(gains, transition)
    whole, drive, start = call(
        response_kernel, [V] * 9, [V] * 3,
        [shape(rows, grid), shape(frames, grid), shape(VEC, grid)],
    )(*partials, final_offset_entries[None], gains, transition, chain, prefix)

    big, small = shape(rows, grid), shape(grid // 2 + VEC, grid)
    held = [pltpu.VMEM((2, rows, grid), F32)]

    def moved(a, axis, to):
        return lax.ppermute(a, axis, [(k, to(k)) for k in range(lax.axis_size(axis))])

    ways = [
        ("c", lambda k: 1 - k), ("z", lambda k: k ^ 1), ("z", lambda k: k ^ 2),
        ("z", lambda k: 7 - k), ("x", lambda k: k ^ 1), ("x", lambda k: k ^ 2),
    ]
    others = [moved(whole, *ways[0])]
    whole, half = call(
        functools.partial(whole_kernel, 0), [V, V], [V, V], [big, small], held
    )(whole, others[0])
    for level in (1, 2, 3):
        mine = moved(half, *ways[level])
        theirs = moved(mine, *ways[0])
        whole, half, other = call(
            functools.partial(halves_kernel, level), [V] * 3, [V] * 3, [big, small, big], held
        )(whole, mine, theirs)
        others.append(other)
    mine = moved(half, *ways[4])
    theirs = moved(mine, *ways[0])
    end, group = call(
        functools.partial(end_kernel, 4), [V] * 3, [V, V], [shape(VEC, grid), big], held
    )(whole, mine, theirs)
    end = moved(end, *ways[5])
    starts, shifts = call(
        starts_kernel, [V] * 6, [V, V], [shape(chains, grid, grid), shape(VEC, grid)],
        [pltpu.VMEM((rows, grid), F32)],
    )(*others, prefix, start)

    share = frames // parts
    filtered, weight, value, send = call(
        final_kernel, [V] * 8, [V] * 4,
        [shape(share, grid)] * 3 + [shape(blocks, 2 * grid)],
        [pltpu.VMEM((frames, grid), F32)] * 3,
    )(end, group, starts, shifts, drive, gains, smooth_gains, transition)
    got = lax.all_to_all(send, TM, 0, 0, tiled=True)
    smoothed = call(smooth_kernel, [V, V, V], V, shape(share, grid))(
        got, weight, value
    )
    return filtered, smoothed


def solution(mesh):
    torus = Mesh(mesh.devices.reshape(4, 8, 2, mesh.shape["mp"]), ("x", "z", "c", "y"))
    return jax.shard_map(
        on_device,
        mesh=torus,
        in_specs=(
            P(TM, None), P(None, "y"), P("y"), P("y", None), P(), P(), P(TM, None), P(TM, None),
        ),
        out_specs=(P((*TM, "y"), None), P((*TM, "y"), None)),
        check_vma=False,
    )
```

time: 100 us -> 87 us (0.87)
  blocking collectives: 43.2 us -> 20.7 us
  waiting for transfers between devices: 11.5 us -> 25.8 us
  matrix products: 3.2 us -> 0 us
  local copies, waits for them, and re-layouts: 1.95 us -> 0.16 us
  other arithmetic: 1.67 us -> 0 us
  Pallas kernels: 13.2 us -> 14.8 us
    all_gather x3 -> x0, blocking collectives: 17.7 us -> none  [the longest x1 8.37 us: on_device(): lax.all_gather(pair, 'z', axis_index_groups=[[2 * k, 2 * k + 1] for k in...]
    ppermute x6 -> x13, waiting for transfers between devices: 10.5 us -> 25.8 us  [the longest x10 25.8 us: moved(): lax.ppermute(a, axis, [(k, to(k)) for k in range(lax.axis_size(axis))])]
    ppermute x6 -> x13, starting transfers between devices: 19 us -> 24.6 us  [the longest x10 18.7 us: moved(): lax.ppermute(a, axis, [(k, to(k)) for k in range(lax.axis_size(axis))])]
    all_to_all x1 -> x0, starting transfers between devices: 5.01 us -> none  [on_device(): lax.all_to_all(jnp.broadcast_to(partial, (parts, frames, grid)), 'y', 0,...]
    all_to_all x1, blocking collectives: 25.5 us -> 20.7 us  [on_device(): got = lax.all_to_all(send, TM, 0, 0, tiled=True)]
    dot_general x1 -> x0, matrix products: 3.2 us -> none  [on_device(): partial = jnp.dot(hidden, output_weight, preferred_element_type=F32)]
    pallas_call x8 -> x10, Pallas kernels: 9.37 us -> 11 us  [the longest x1 2.85 us: on_device(): call(network_kernel, [H] * 4, V, shape(frames, grid), [pltpu.VMEM(feature...]
    unnamed x11 -> x9, local copies, waits for them, and re-layouts: 1.04 us -> 0.03 us
  transfers between devices with their start and end apart: 7 -> 13, of which waited for: 6 -> 10; matrix products, arithmetic and copies ran while one was open for 0% -> 0% of each run, Pallas kernels for 4% -> 5%
where the time goes in v1:
time: 87 us; the launch traced here: 86.9 us
  waiting for transfers between devices  25.8 us (30%)
  starting transfers between devices  24.6 us (28%)
  blocking collectives  20.7 us (24%)
  Pallas kernels  14.8 us (17%)
    ppermute x10, waiting for transfers between devices, moved(): lax.ppermute(a, axis, [(k, to(k)) for k in range(lax.axis_size(axis))])  25.8 us
    all_to_all x1, blocking collectives, on_device(): got = lax.all_to_all(send, TM, 0, 0, tiled=True)  20.7 us
    ppermute x10, starting transfers between devices, moved(): lax.ppermute(a, axis, [(k, to(k)) for k in range(lax.axis_size(axis))])  18.7 us
    ppermute x3, starting transfers between devices, on_device(): lax.ppermute(partial, 'y', [(k, (k + s) % parts) for k in range(parts)])  5.89 us
    pallas_call x1, Pallas kernels, on_device(): call(block_kernel, [V, V], [V, V], [shape(chains, grid, grid), shape(chai...  3.87 us
    pallas_call x1, Pallas kernels, on_device(): call(network_kernel, [H] * 4, V, shape(frames, grid), [pltpu.VMEM(feature...  2.85 us
    pallas_call x1, Pallas kernels, on_device(): call(final_kernel, [V] * 8, [V] * 4, [shape(share, grid)] * 3 + [shape(bl...  2.63 us
    pallas_call x1, Pallas kernels, on_device(): call(response_kernel, [V] * 9, [V] * 3, [shape(rows, grid), shape(frames,...  1.98 us
  transfers between devices with their start and end apart: 13, of which 10 were waited for; matrix products, arithmetic and copies ran while one was open for 0% of the time, Pallas kernels for 5%

profile of v1, /device:TPU:1, one launch (start us, length us, event | category | flops | bytes accessed | tf_op | source)
XLA Modules:
  0.0 86.9 jit_solution(8395679467549700351)
XLA Ops:
  0.6 0.0 copy-start.1
  0.6 0.0 copy-start
  0.7 0.0 copy-start.3
  0.7 2.9 %shard_map.95.one_ref = f32[32,256]{1,0:T(8,128)S(1)} custom-call(bf16[32,2048]{1,0:T(8,128)(2,1)} %features_hbm.1, bf16[2048,1024]{1,0:T(8,128)(2,1)} %w_in_hbm.1, f32[1,1024]{1,0:T(1,128)} %bitcast.9, bf16[1024,256]{1,0:T(8,128)(2,1)} %out_weight_hbm.1), custom_call_target="tpu_custom_call" | custom-call | tf_op jit(solution)/shard_map/pallas_call | solution.py:268
  3.5 0.0 copy-start.2
  3.5 2.2 %collective-permute-start = (f32[32,256]{1,0:T(8,128)S(1)}, f32[32,256]{1,0:T(8,128)S(1)}, u32[]{:S(2)}, u32[]{:S(2)}) collective-permute-start(f32[32,256]{1,0:T(8,128)S(1)} %shard_map.95.one_ref), channel_id=1, source_target_pairs={{0,1},{1,2},{2,3},{3,0},{4,5},{5,6},{6,7},{7,4},{8,9},{9,10},{10,1... | collective-permute-start | bytes 98312 | tf_op jit(solution)/shard_map/ppermute | solution.py:277
  5.7 2.6 %collective-permute-start.1 = (f32[32,256]{1,0:T(8,128)S(1)}, f32[32,256]{1,0:T(8,128)S(1)}, u32[]{:S(2)}, u32[]{:S(2)}) collective-permute-start(f32[32,256]{1,0:T(8,128)S(1)} %shard_map.95.one_ref), channel_id=1, source_target_pairs={{0,2},{1,3},{2,0},{3,1},{4,6},{5,7},{6,4},{7,5},{8,10},{9,11},{10,... | collective-permute-start | bytes 98312 | tf_op jit(solution)/shard_map/ppermute | solution.py:277
  8.4 1.1 %collective-permute-start.2 = (f32[32,256]{1,0:T(8,128)S(1)}, f32[32,256]{1,0:T(8,128)S(1)}, u32[]{:S(2)}, u32[]{:S(2)}) collective-permute-start(f32[32,256]{1,0:T(8,128)S(1)} %shard_map.95.one_ref), channel_id=1, source_target_pairs={{0,3},{1,0},{2,1},{3,2},{4,7},{5,4},{6,5},{7,6},{8,11},{9,8},{10,9... | collective-permute-start | bytes 98312 | tf_op jit(solution)/shard_map/ppermute | solution.py:277
  9.4 0.0 copy-done.1
  9.4 0.0 copy-done
  9.4 3.9 %shard_map.96 = (f32[4,256,256]{2,1,0:T(8,128)S(1)}, f32[4,256,256]{2,1,0:T(8,128)S(1)}) custom-call(f32[32,256]{1,0:T(8,128)S(1)} %copy-done.1, f32[256,256]{1,0:T(8,128)S(1)} %copy-done), custom_call_target="tpu_custom_call" | custom-call | tf_op jit(solution)/shard_map/pallas_call | solution.py:281
  13.3 0.0 collective-permute-done.two_ref
  13.3 0.0 collective-permute-done.1.three_ref
  13.3 0.0 collective-permute-done.2.four_ref
  13.3 0.0 copy-done.3
  13.4 2.0 %shard_map.97 = (f32[264,256]{1,0:T(8,128)S(1)}, f32[32,256]{1,0:T(8,128)S(1)}, f32[8,256]{1,0:T(8,128)S(1)}) custom-call(f32[32,256]{1,0:T(8,128)S(1)} %shard_map.95.one_ref, f32[32,256]{1,0:T(8,128)S(1)} %collective-permute-done.two_ref, f32[32,256]{1,0:T(8,128)S(1)} %collective-permute-done.1.three_ref, f32[32,256]{1,0:T(8,128)S(1)} %collective-permute-done.2.four_ref, ...), custom_call_target="tpu_custom_call" | custom-call | tf_op jit(solution)/shard_map/pallas_call | solution.py:285
  15.3 1.5 %collective-permute-start.3 = (f32[264,256]{1,0:T(8,128)S(1)}, f32[264,256]{1,0:T(8,128)S(1)}, u32[]{:S(2)}, u32[]{:S(2)}) collective-permute-start(f32[264,256]{1,0:T(8,128)S(1)} %get-tuple-element.28.own_ref), channel_id=1, source_target_pairs={{0,4},{4,0},{1,5},{5,1},{2,6},{6,2},{3,7},{7,3},{8,12},{12,8},{9,1... | collective-permute-start | bytes 811016 | tf_op jit(solution)/shard_map/ppermute | solution.py:294
  16.9 1.2 %collective-permute-done.3.other_ref.refs_0_ = f32[264,256]{1,0:T(8,128)S(1)} collective-permute-done((f32[264,256]{1,0:T(8,128)S(1)}, f32[264,256]{1,0:T(8,128)S(1)}, u32[]{:S(2)}, u32[]{:S(2)}) %collective-permute-start.3) | collective-permute-done | bytes 270368 | tf_op jit(solution)/shard_map/ppermute | solution.py:294
  18.0 0.4 shard_map.98
  18.4 1.7 %collective-permute-start.4 = (f32[136,256]{1,0:T(8,128)S(1)}, f32[136,256]{1,0:T(8,128)S(1)}, u32[]{:S(2)}, u32[]{:S(2)}) collective-permute-start(f32[136,256]{1,0:T(8,128)S(1)} %get-tuple-element.30), channel_id=1, source_target_pairs={{0,8},{8,0},{16,24},{24,16},{32,40},{40,32},{48,56},{56,48},{1,9},... | collective-permute-start | bytes 417800 | tf_op jit(solution)/shard_map/ppermute | solution.py:294
  20.1 3.6 %collective-permute-done.4.mine_ref = f32[136,256]{1,0:T(8,128)S(1)} collective-permute-done((f32[136,256]{1,0:T(8,128)S(1)}, f32[136,256]{1,0:T(8,128)S(1)}, u32[]{:S(2)}, u32[]{:S(2)}) %collective-permute-start.4) | collective-permute-done | bytes 139296 | tf_op jit(solution)/shard_map/ppermute | solution.py:294
  23.8 1.0 %collective-permute-start.5 = (f32[136,256]{1,0:T(8,128)S(1)}, f32[136,256]{1,0:T(8,128)S(1)}, u32[]{:S(2)}, u32[]{:S(2)}) collective-permute-start(f32[136,256]{1,0:T(8,128)S(1)} %collective-permute-done.4.mine_ref), channel_id=1, source_target_pairs={{0,4},{4,0},{1,5},{5,1},{2,6},{6,2},{3,7},{7,3},{8,12},{12,8},{9,1... | collective-permute-start | bytes 417800 | tf_op jit(solution)/shard_map/ppermute | solution.py:294
  24.8 1.0 %collective-permute-done.5.theirs_ref = f32[136,256]{1,0:T(8,128)S(1)} collective-permute-done((f32[136,256]{1,0:T(8,128)S(1)}, f32[136,256]{1,0:T(8,128)S(1)}, u32[]{:S(2)}, u32[]{:S(2)}) %collective-permute-start.5) | collective-permute-done | bytes 139296 | tf_op jit(solution)/shard_map/ppermute | solution.py:294
  25.8 0.4 shard_map.99
  26.2 3.1 %collective-permute-start.6 = (f32[136,256]{1,0:T(8,128)S(1)}, f32[136,256]{1,0:T(8,128)S(1)}, u32[]{:S(2)}, u32[]{:S(2)}) collective-permute-start(f32[136,256]{1,0:T(8,128)S(1)} %get-tuple-element.32), channel_id=1, source_target_pairs={{0,16},{8,24},{16,0},{24,8},{32,48},{40,56},{48,32},{56,40},{1,17}... | collective-permute-start | bytes 417800 | tf_op jit(solution)/shard_map/ppermute | solution.py:294
  29.2 6.7 %collective-permute-done.6.mine_ref = f32[136,256]{1,0:T(8,128)S(1)} collective-permute-done((f32[136,256]{1,0:T(8,128)S(1)}, f32[136,256]{1,0:T(8,128)S(1)}, u32[]{:S(2)}, u32[]{:S(2)}) %collective-permute-start.6) | collective-permute-done | bytes 139296 | tf_op jit(solution)/shard_map/ppermute | solution.py:294
  36.0 0.9 collective-permute-start.7
  36.9 1.0 %collective-permute-done.7.theirs_ref = f32[136,256]{1,0:T(8,128)S(1)} collective-permute-done((f32[136,256]{1,0:T(8,128)S(1)}, f32[136,256]{1,0:T(8,128)S(1)}, u32[]{:S(2)}, u32[]{:S(2)}) %collective-permute-start.7) | collective-permute-done | bytes 139296 | tf_op jit(solution)/shard_map/ppermute | solution.py:294
  37.8 0.4 shard_map.100
  38.3 4.8 %collective-permute-start.8 = (f32[136,256]{1,0:T(8,128)S(1)}, f32[136,256]{1,0:T(8,128)S(1)}, u32[]{:S(2)}, u32[]{:S(2)}) collective-permute-start(f32[136,256]{1,0:T(8,128)S(1)} %get-tuple-element.34), channel_id=1, source_target_pairs={{0,56},{8,48},{16,40},{24,32},{32,24},{40,16},{48,8},{56,0},{1,57}... | collective-permute-start | bytes 417800 | tf_op jit(solution)/shard_map/ppermute | solution.py:294
  43.1 6.2 %collective-permute-done.8.mine_ref = f32[136,256]{1,0:T(8,128)S(1)} collective-permute-done((f32[136,256]{1,0:T(8,128)S(1)}, f32[136,256]{1,0:T(8,128)S(1)}, u32[]{:S(2)}, u32[]{:S(2)}) %collective-permute-start.8) | collective-permute-done | bytes 139296 | tf_op jit(solution)/shard_map/ppermute | solution.py:294
  49.3 0.4 collective-permute-start.9
  49.7 1.0 %collective-permute-done.9.theirs_ref = f32[136,256]{1,0:T(8,128)S(1)} collective-permute-done((f32[136,256]{1,0:T(8,128)S(1)}, f32[136,256]{1,0:T(8,128)S(1)}, u32[]{:S(2)}, u32[]{:S(2)}) %collective-permute-start.9) | collective-permute-done | bytes 139296 | tf_op jit(solution)/shard_map/ppermute | solution.py:294
  50.7 0.4 shard_map.101
  51.1 1.3 %collective-permute-start.10 = (f32[136,256]{1,0:T(8,128)S(1)}, f32[136,256]{1,0:T(8,128)S(1)}, u32[]{:S(2)}, u32[]{:S(2)}) collective-permute-start(f32[136,256]{1,0:T(8,128)S(1)} %get-tuple-element.36), channel_id=1, source_target_pairs={{0,64},{64,0},{128,192},{192,128},{1,65},{65,1},{129,193},{193,129... | collective-permute-start | bytes 417800 | tf_op jit(solution)/shard_map/ppermute | solution.py:294
  52.4 3.7 %collective-permute-done.10.mine_ref = f32[136,256]{1,0:T(8,128)S(1)} collective-permute-done((f32[136,256]{1,0:T(8,128)S(1)}, f32[136,256]{1,0:T(8,128)S(1)}, u32[]{:S(2)}, u32[]{:S(2)}) %collective-permute-start.10) | collective-permute-done | bytes 139296 | tf_op jit(solution)/shard_map/ppermute | solution.py:294
  56.1 1.2 %collective-permute-start.11 = (f32[136,256]{1,0:T(8,128)S(1)}, f32[136,256]{1,0:T(8,128)S(1)}, u32[]{:S(2)}, u32[]{:S(2)}) collective-permute-start(f32[136,256]{1,0:T(8,128)S(1)} %collective-permute-done.10.mine_ref), channel_id=1, source_target_pairs={{0,4},{4,0},{1,5},{5,1},{2,6},{6,2},{3,7},{7,3},{8,12},{12,8},{9,1... | collective-permute-start | bytes 417800 | tf_op jit(solution)/shard_map/ppermute | solution.py:294
  57.3 1.0 %collective-permute-done.11.theirs_ref = f32[136,256]{1,0:T(8,128)S(1)} collective-permute-done((f32[136,256]{1,0:T(8,128)S(1)}, f32[136,256]{1,0:T(8,128)S(1)}, u32[]{:S(2)}, u32[]{:S(2)}) %collective-permute-start.11) | collective-permute-done | bytes 139296 | tf_op jit(solution)/shard_map/ppermute | solution.py:294
  58.3 0.3 shard_map.102
  58.5 2.8 %collective-permute-start.12 = (f32[8,256]{1,0:T(8,128)S(1)}, f32[8,256]{1,0:T(8,128)S(1)}, u32[]{:S(2)}, u32[]{:S(2)}) collective-permute-start(f32[8,256]{1,0:T(8,128)S(1)} %get-tuple-element.37), channel_id=1, source_target_pairs={{0,128},{64,192},{128,0},{192,64},{1,129},{65,193},{129,1},{193,65... | collective-permute-start | bytes 24584 | tf_op jit(solution)/shard_map/ppermute | solution.py:294
  61.3 0.8 shard_map.103
  62.1 0.4 collective-permute-done.12.end_ref
  62.5 0.0 copy-done.2
  62.5 2.6 %shard_map.104 = (f32[8,256]{1,0:T(8,128)}, f32[8,256]{1,0:T(8,128)S(1)}, f32[8,256]{1,0:T(8,128)S(1)}, f32[64,512]{1,0:T(8,128)S(1)}) custom-call(f32[8,256]{1,0:T(8,128)S(1)} %collective-permute-done.12.end_ref, f32[264,256]{1,0:T(8,128)S(1)} %get-tuple-element.38.group_ref, f32[4,256,256]{2,1,0:T(8,128)S(1)} %get-tuple-element.43.starts_ref, ...), custom_call_target="tpu_custom_call" | custom-call | tf_op jit(solution)/shard_map/pallas_call | solution.py:323
  65.2 0.1 copy.10
  65.3 20.7 %all_to_all.11 = f32[64,1,512]{2,1,0:T(1,128)S(1)} all-to-all(f32[64,1,512]{2,1,0:T(1,128)S(1)} %copy.10), channel_id=1, replica_groups=mesh['x'=4,'z'=8,'c'=2,'y'=4] {'x','z','c'}, dimensions={0} | all-to-all | bytes 262144 | tf_op jit(solution)/shard_map/all_to_all | solution.py:328
  86.0 0.8 shard_map.105
  (1 shorter events, 0.0 us)
Async XLA Ops:
  0.6 8.8 %copy-start.1 = (f32[32,256]{1,0:T(8,128)S(1)}, f32[32,256]{1,0:T(8,128)}, u32[]{:S(2)}) copy-start(f32[32,256]{1,0:T(8,128)} %gains_ref.5) | copy-start | bytes 98308
  0.6 8.8 %copy-start = (f32[256,256]{1,0:T(8,128)S(1)}, f32[256,256]{1,0:T(8,128)}, u32[]{:S(2)}) copy-start(f32[256,256]{1,0:T(8,128)} %transition_ref.5) | copy-start | bytes 786436
  0.7 12.7 %copy-start.3 = (f32[256]{0:T(256)S(1)}, f32[256]{0:T(256)}, u32[]{:S(2)}) copy-start(f32[256]{0:T(256)} %param.12) | copy-start | bytes 3076
  3.5 59.0 %copy-start.2 = (f32[32,256]{1,0:T(8,128)S(1)}, f32[32,256]{1,0:T(8,128)}, u32[]{:S(2)}) copy-start(f32[32,256]{1,0:T(8,128)} %smooth_ref.1) | copy-start | bytes 98308
  3.5 9.8 %collective-permute-start = (f32[32,256]{1,0:T(8,128)S(1)}, f32[32,256]{1,0:T(8,128)S(1)}, u32[]{:S(2)}, u32[]{:S(2)}) collective-permute-start(f32[32,256]{1,0:T(8,128)S(1)} %shard_map.95.one_ref), channel_id=1, source_target_pairs={{0,1},{1,2},{2,3},{3,0},{4,5},{5,6},{6,7},{7,4},{8,9},{9,10},{10,1... | collective-permute-start | bytes 98312 | tf_op jit(solution)/shard_map/ppermute | solution.py:277
  5.7 7.6 %collective-permute-start.1 = (f32[32,256]{1,0:T(8,128)S(1)}, f32[32,256]{1,0:T(8,128)S(1)}, u32[]{:S(2)}, u32[]{:S(2)}) collective-permute-start(f32[32,256]{1,0:T(8,128)S(1)} %shard_map.95.one_ref), channel_id=1, source_target_pairs={{0,2},{1,3},{2,0},{3,1},{4,6},{5,7},{6,4},{7,5},{8,10},{9,11},{10,... | collective-permute-start | bytes 98312 | tf_op jit(solution)/shard_map/ppermute | solution.py:277
  8.4 5.0 %collective-permute-start.2 = (f32[32,256]{1,0:T(8,128)S(1)}, f32[32,256]{1,0:T(8,128)S(1)}, u32[]{:S(2)}, u32[]{:S(2)}) collective-permute-start(f32[32,256]{1,0:T(8,128)S(1)} %shard_map.95.one_ref), channel_id=1, source_target_pairs={{0,3},{1,0},{2,1},{3,2},{4,7},{5,4},{6,5},{7,6},{8,11},{9,8},{10,9... | collective-permute-start | bytes 98312 | tf_op jit(solution)/shard_map/ppermute | solution.py:277
  15.3 2.7 %collective-permute-start.3 = (f32[264,256]{1,0:T(8,128)S(1)}, f32[264,256]{1,0:T(8,128)S(1)}, u32[]{:S(2)}, u32[]{:S(2)}) collective-permute-start(f32[264,256]{1,0:T(8,128)S(1)} %get-tuple-element.28.own_ref), channel_id=1, source_target_pairs={{0,4},{4,0},{1,5},{5,1},{2,6},{6,2},{3,7},{7,3},{8,12},{12,8},{9,1... | collective-permute-start | bytes 811016 | tf_op jit(solution)/shard_map/ppermute | solution.py:294
  18.4 5.4 %collective-permute-start.4 = (f32[136,256]{1,0:T(8,128)S(1)}, f32[136,256]{1,0:T(8,128)S(1)}, u32[]{:S(2)}, u32[]{:S(2)}) collective-permute-start(f32[136,256]{1,0:T(8,128)S(1)} %get-tuple-element.30), channel_id=1, source_target_pairs={{0,8},{8,0},{16,24},{24,16},{32,40},{40,32},{48,56},{56,48},{1,9},... | collective-permute-start | bytes 417800 | tf_op jit(solution)/shard_map/ppermute | solution.py:294
  23.8 2.0 %collective-permute-start.5 = (f32[136,256]{1,0:T(8,128)S(1)}, f32[136,256]{1,0:T(8,128)S(1)}, u32[]{:S(2)}, u32[]{:S(2)}) collective-permute-start(f32[136,256]{1,0:T(8,128)S(1)} %collective-permute-done.4.mine_ref), channel_id=1, source_target_pairs={{0,4},{4,0},{1,5},{5,1},{2,6},{6,2},{3,7},{7,3},{8,12},{12,8},{9,1... | collective-permute-start | bytes 417800 | tf_op jit(solution)/shard_map/ppermute | solution.py:294
  26.2 9.8 %collective-permute-start.6 = (f32[136,256]{1,0:T(8,128)S(1)}, f32[136,256]{1,0:T(8,128)S(1)}, u32[]{:S(2)}, u32[]{:S(2)}) collective-permute-start(f32[136,256]{1,0:T(8,128)S(1)} %get-tuple-element.32), channel_id=1, source_target_pairs={{0,16},{8,24},{16,0},{24,8},{32,48},{40,56},{48,32},{56,40},{1,17}... | collective-permute-start | bytes 417800 | tf_op jit(solution)/shard_map/ppermute | solution.py:294
  36.0 1.9 %collective-permute-start.7 = (f32[136,256]{1,0:T(8,128)S(1)}, f32[136,256]{1,0:T(8,128)S(1)}, u32[]{:S(2)}, u32[]{:S(2)}) collective-permute-start(f32[136,256]{1,0:T(8,128)S(1)} %collective-permute-done.6.mine_ref), channel_id=1, source_target_pairs={{0,4},{4,0},{1,5},{5,1},{2,6},{6,2},{3,7},{7,3},{8,12},{12,8},{9,1... | collective-permute-start | bytes 417800 | tf_op jit(solution)/shard_map/ppermute | solution.py:294
  38.3 11.0 %collective-permute-start.8 = (f32[136,256]{1,0:T(8,128)S(1)}, f32[136,256]{1,0:T(8,128)S(1)}, u32[]{:S(2)}, u32[]{:S(2)}) collective-permute-start(f32[136,256]{1,0:T(8,128)S(1)} %get-tuple-element.34), channel_id=1, source_target_pairs={{0,56},{8,48},{16,40},{24,32},{32,24},{40,16},{48,8},{56,0},{1,57}... | collective-permute-start | bytes 417800 | tf_op jit(solution)/shard_map/ppermute | solution.py:294
  49.3 1.4 %collective-permute-start.9 = (f32[136,256]{1,0:T(8,128)S(1)}, f32[136,256]{1,0:T(8,128)S(1)}, u32[]{:S(2)}, u32[]{:S(2)}) collective-permute-start(f32[136,256]{1,0:T(8,128)S(1)} %collective-permute-done.8.mine_ref), channel_id=1, source_target_pairs={{0,4},{4,0},{1,5},{5,1},{2,6},{6,2},{3,7},{7,3},{8,12},{12,8},{9,1... | collective-permute-start | bytes 417800 | tf_op jit(solution)/shard_map/ppermute | solution.py:294
  51.1 5.0 %collective-permute-start.10 = (f32[136,256]{1,0:T(8,128)S(1)}, f32[136,256]{1,0:T(8,128)S(1)}, u32[]{:S(2)}, u32[]{:S(2)}) collective-permute-start(f32[136,256]{1,0:T(8,128)S(1)} %get-tuple-element.36), channel_id=1, source_target_pairs={{0,64},{64,0},{128,192},{192,128},{1,65},{65,1},{129,193},{193,129... | collective-permute-start | bytes 417800 | tf_op jit(solution)/shard_map/ppermute | solution.py:294
  56.1 2.2 %collective-permute-start.11 = (f32[136,256]{1,0:T(8,128)S(1)}, f32[136,256]{1,0:T(8,128)S(1)}, u32[]{:S(2)}, u32[]{:S(2)}) collective-permute-start(f32[136,256]{1,0:T(8,128)S(1)} %collective-permute-done.10.mine_ref), channel_id=1, source_target_pairs={{0,4},{4,0},{1,5},{5,1},{2,6},{6,2},{3,7},{7,3},{8,12},{12,8},{9,1... | collective-permute-start | bytes 417800 | tf_op jit(solution)/shard_map/ppermute | solution.py:294
  58.5 4.0 %collective-permute-start.12 = (f32[8,256]{1,0:T(8,128)S(1)}, f32[8,256]{1,0:T(8,128)S(1)}, u32[]{:S(2)}, u32[]{:S(2)}) collective-permute-start(f32[8,256]{1,0:T(8,128)S(1)} %get-tuple-element.37), channel_id=1, source_target_pairs={{0,128},{64,192},{128,0},{192,64},{1,129},{65,193},{129,1},{193,65... | collective-permute-start | bytes 24584 | tf_op jit(solution)/shard_map/ppermute | solution.py:294

commit v2 on v1

--- a/solution.py
+++ b/solution.py
@@ -8,9 +8,11 @@
 from jax.sharding import Mesh
 from jax.sharding import PartitionSpec as P
 
-TM = ("x", "z", "c")
+Z = ("q", "k")
+TM = ("x", "q", "k", "c")
 F32, BF16 = jnp.float32, jnp.bfloat16
 SUB = 8
+MERGED = 2
 VEC = 8
 
 
@@ -19,18 +21,18 @@
     return high, (a - high.astype(F32)).astype(BF16)
 
 
-def left(a):
+def right(b):
+    return pieces(b)
+
+
+def times(a, b):
     high, low = pieces(a)
-    return jnp.concatenate([high, low, high], axis=1)
-
-
-def right(b):
-    high, low = pieces(b)
-    return jnp.concatenate([high, high, low], axis=0)
-
-
-def times(a, b3):
-    return jnp.dot(left(a), b3, preferred_element_type=F32)
+    rows = a.shape[0]
+    if rows > 16:
+        both = jnp.concatenate([high, low, high], axis=1)
+        return jnp.dot(both, jnp.concatenate([b[0], b[0], b[1]], axis=0), preferred_element_type=F32)
+    top = jnp.dot(jnp.concatenate([high, low], axis=0), b[0], preferred_element_type=F32)
+    return (top[:rows] + top[rows:]) + jnp.dot(high, b[1], preferred_element_type=F32)
 
 
 def each(ref, t, chains):
@@ -41,7 +43,7 @@
     if level == 0:
         return lax.axis_index("c")
     if level < 4:
-        return (lax.axis_index("z") >> (level - 1)) & 1
+        return (lax.axis_index(Z) >> (level - 1)) & 1
     return (lax.axis_index("x") >> (level - 4)) & 1
 
 
@@ -123,6 +125,102 @@
     return times(earlier, right(later[:grid])) + added
 
 
+def closed(smooth_ref):
+    frames, grid = smooth_ref.shape
+    last = lax.axis_index(TM) == lax.axis_size(TM) - 1
+    row = lax.broadcasted_iota(jnp.int32, (frames, grid), 0)
+    return jnp.where((row == frames - 1) & last, 0.0, smooth_ref[...])
+
+
+def summary_kernel(
+    gains_ref, smooth_ref, transition_ref, drive_ref, prefix_ref, start_ref,
+    sum_ref, walk, total, reach_ref,
+):
+    chains, grid = prefix_ref.shape[0], prefix_ref.shape[2]
+    flipped = transition_ref[...].T
+    step = right(flipped)
+    weight = closed(smooth_ref)
+    reach = jnp.ones((1, grid), F32)
+    for t in range(weight.shape[0]):
+        reach_ref[t : t + 1, :] = reach
+        reach = reach * weight[t : t + 1]
+    whole_reach = reach
+    for j in range(chains):
+        row = SUB * j
+        walk[j, 0:grid, :] = flipped * (1.0 - gains_ref[row : row + 1, :])
+        walk[j, grid:, :] = padded(drive_ref[row : row + 1, :])
+    for t in range(SUB):
+        for j in range(chains):
+            row = SUB * j + t
+            now = walk[j]
+            moved = times(now, step)
+            worth = (now - moved * weight[row : row + 1]) * reach_ref[row : row + 1, :]
+            total[j] = worth if t == 0 else total[j] + worth
+            if t < SUB - 1:
+                keep = 1.0 - gains_ref[row + 1 : row + 2, :]
+                walk[j, 0:grid, :] = moved[:grid] * keep
+                walk[j, grid:, :] = moved[grid:] * keep + padded(drive_ref[row + 1 : row + 2, :])
+    slope, rest = total[0, 0:grid, :], total[0, grid : grid + 1, :]
+    for j in range(1, chains):
+        entry = jnp.concatenate([prefix_ref[j - 1], padded(start_ref[j : j + 1, :])], axis=0)
+        moved = times(entry, right(total[j, 0:grid, :]))
+        slope = slope + moved[:grid]
+        rest = rest + moved[grid : grid + 1] + total[j, grid : grid + 1, :]
+    sum_ref[0:grid, :] = slope
+    sum_ref[grid:, :] = jnp.concatenate(
+        [rest, whole_reach, jnp.zeros((VEC - 2, grid), F32)], axis=0
+    )
+
+
+def merged_kernel(level, *refs):
+    own_ref, other_ref, own_sum_ref, other_sum_ref, *before, sum_ref, later_ref = refs
+    grid = own_ref.shape[1]
+    upper = bit(level)
+
+    def put(to_ref, slope, rest, reach):
+        to_ref[0:grid, :] = slope
+        to_ref[grid:, :] = jnp.concatenate([rest, reach, jnp.zeros((VEC - 2, grid), F32)], axis=0)
+
+    def joined(first_ref, low_ref, high_ref):
+        moved = times(first_ref[...], right(high_ref[0:grid, :]))
+        slope, rest = moved[:grid], moved[grid : grid + 1] + high_ref[grid : grid + 1, :]
+        low, high = low_ref[grid + 1 : grid + 2, :], high_ref[grid + 1 : grid + 2, :]
+        put(
+            sum_ref, low_ref[0:grid, :] + slope * low,
+            low_ref[grid : grid + 1, :] + rest * low, low * high,
+        )
+        return slope, rest, high
+
+    @pl.when(upper == 0)
+    def _():
+        slope, rest, high = joined(own_ref, own_sum_ref, other_sum_ref)
+        if before:
+            old = before[0]
+            reach = old[grid + 1 : grid + 2, :]
+            slope = old[0:grid, :] + slope * reach
+            rest = old[grid : grid + 1, :] + rest * reach
+            high = reach * high
+        put(later_ref, slope, rest, high)
+
+    @pl.when(upper > 0)
+    def _():
+        joined(other_ref, other_sum_ref, own_sum_ref)
+        if before:
+            old = before[0]
+            moved = times(other_ref[...], right(old[0:grid, :]))
+            put(
+                later_ref, moved[:grid], moved[grid : grid + 1] + old[grid : grid + 1, :],
+                old[grid + 1 : grid + 2, :],
+            )
+        else:
+            nothing = jnp.zeros((grid, grid), F32)
+            put(later_ref, nothing, nothing[0:1], nothing[0:1] + 1.0)
+
+
+def padded(row):
+    return jnp.concatenate([row, jnp.zeros((VEC - 1, row.shape[1]), F32)], axis=0)
+
+
 def ordered(held, own, other, upper):
     held[0] = own
     held[1] = other
@@ -165,13 +263,21 @@
 
 
 def starts_kernel(*refs):
-    others, (prefix_ref, start_ref, starts_ref, shifts_ref, held) = refs[:4], refs[4:]
+    others, (prefix_ref, start_ref, sum_ref, later_ref, starts_ref, shifts_ref, held) = refs[:4], refs[4:]
     chains, grid = prefix_ref.shape[0], prefix_ref.shape[2]
     top = others[3]
     row = lax.broadcasted_iota(jnp.int32, top.shape, 0)
     column = lax.broadcasted_iota(jnp.int32, top.shape, 1)
     held[...] = jnp.where(bit(3) > 0, top[...], jnp.where(row == column, 1.0, 0.0))
+    tail = []
     for level in (2, 1, 0):
+        if level == MERGED - 1:
+            for k, part_ref in enumerate((sum_ref, later_ref)):
+                moved = times(held[...], right(part_ref[0:grid, :]))
+                starts_ref[chains + k] = moved[:grid]
+                tail.append(moved[grid : grid + 1] + part_ref[grid : grid + 1, :])
+                tail.append(part_ref[grid + 1 : grid + 2, :])
+
         @pl.when(bit(level) > 0)
         def _():
             held[...] = after(held[...], others[level][...])
@@ -181,7 +287,17 @@
         moved = times(held[...], right(prefix_ref[j - 1]))
         starts_ref[j] = moved[:grid]
         rows.append(moved[grid : grid + 1] + start_ref[j : j + 1, :])
-    shifts_ref[...] = jnp.concatenate([*rows, jnp.zeros((VEC - chains, grid), F32)], axis=0)
+    shifts_ref[...] = jnp.concatenate([*rows, *tail], axis=0)
+
+
+def send_kernel(end_ref, group_ref, starts_ref, shifts_ref, state_ref, send_ref):
+    chains = starts_ref.shape[0] - 2
+    state = jnp.where(bit(5) > 0, end_ref[...], 0.0)
+    state = jnp.where(bit(4) > 0, advance(state, group_ref[...]), state)
+    state_ref[...] = state
+    v = times(state, right(starts_ref[chains]))[0:1] + shifts_ref[chains : chains + 1, :]
+    d = shifts_ref[chains + 1 : chains + 2, :]
+    send_ref[...] = jnp.broadcast_to(jnp.concatenate([d, v], axis=1)[None], send_ref.shape)
 
 
 def advance(state, whole):
@@ -190,16 +306,14 @@
 
 
 def final_kernel(
-    end_ref, group_ref, starts_ref, shifts_ref, drive_ref, gains_ref, smooth_ref, transition_ref,
-    filtered_ref, weight_ref, value_ref, send_ref, found, scan_d, scan_v,
+    state_ref, starts_ref, shifts_ref, drive_ref, gains_ref, smooth_ref, transition_ref,
+    filtered_ref, weight_ref, value_ref, found, scan_d, scan_v,
 ):
-    chains = starts_ref.shape[0]
-    frames, grid = drive_ref.shape
+    chains = starts_ref.shape[0] - 2
+    frames = drive_ref.shape[0]
     part = lax.axis_index("y")
-    last = lax.axis_index(TM) == lax.axis_size(TM) - 1
     step = right(transition_ref[...].T)
-    state = jnp.where(bit(5) > 0, end_ref[...], 0.0)
-    state = jnp.where(bit(4) > 0, advance(state, group_ref[...]), state)
+    state = state_ref[...]
     rows = [times(state, right(starts_ref[j]))[0:1] for j in range(chains)]
     now = jnp.concatenate(rows, axis=0) + shifts_ref[0:chains, :]
     for t in range(SUB):
@@ -207,9 +321,7 @@
         now = times(now, step) * keep + each(drive_ref, t, chains)
         for j in range(chains):
             found[SUB * j + t : SUB * j + t + 1, :] = now[j : j + 1]
-    weight = smooth_ref[...]
-    row = lax.broadcasted_iota(jnp.int32, (frames, grid), 0)
-    weight = jnp.where((row == frames - 1) & last, 0.0, weight)
+    weight = closed(smooth_ref)
     value = found[...] - weight * times(found[...], step)
     d, v = weight[frames - 1 : frames], value[frames - 1 : frames]
     scan_d[frames - 1 : frames, :] = d
@@ -222,15 +334,15 @@
     share = filtered_ref.shape[0]
     mine = pl.ds(pl.multiple_of(part * share, share), share)
     filtered_ref[...] = found[mine, :]
-    weight_ref[...] = scan_d[mine, :]
-    value_ref[...] = scan_v[mine, :]
-    send_ref[...] = jnp.broadcast_to(jnp.concatenate([d, v], axis=1), send_ref.shape)
+    later = times(state, right(starts_ref[chains + 1]))[0:1] + shifts_ref[chains + 2 : chains + 3, :]
+    weight_ref[...] = scan_d[mine, :] * shifts_ref[chains + 3 : chains + 4, :]
+    value_ref[...] = scan_d[mine, :] * later + scan_v[mine, :]
 
 
 def smooth_kernel(got_ref, weight_ref, value_ref, smoothed_ref):
     blocks = got_ref.shape[0]
     grid = weight_ref.shape[1]
-    here = lax.axis_index(TM)
+    here = lax.axis_index(TM) >> MERGED
     row = lax.broadcasted_iota(jnp.int32, (blocks, grid), 0)
     d = jnp.where(row > here, got_ref[:, :grid], 1.0)
     v = jnp.where(row > here, got_ref[:, grid:], 0.0)
@@ -261,7 +373,8 @@
     frames, grid = gains.shape
     chains = frames // SUB
     rows = grid + VEC
-    blocks = lax.axis_size(TM)
+    among = TM[: len(TM) - MERGED]
+    blocks = lax.axis_size(among)
     parts = lax.axis_size("y")
     H = pl.BlockSpec(memory_space=pltpu.HBM)
     units = w_in.shape[1]
@@ -294,38 +407,59 @@
         return lax.ppermute(a, axis, [(k, to(k)) for k in range(lax.axis_size(axis))])
 
     ways = [
-        ("c", lambda k: 1 - k), ("z", lambda k: k ^ 1), ("z", lambda k: k ^ 2),
-        ("z", lambda k: 7 - k), ("x", lambda k: k ^ 1), ("x", lambda k: k ^ 2),
+        ("c", lambda k: 1 - k), (Z, lambda k: k ^ 1), (Z, lambda k: k ^ 2),
+        (Z, lambda k: 7 - k), ("x", lambda k: k ^ 1), ("x", lambda k: k ^ 2),
     ]
+    wholes = [whole]
     others = [moved(whole, *ways[0])]
     whole, half = call(
         functools.partial(whole_kernel, 0), [V, V], [V, V], [big, small], held
     )(whole, others[0])
     for level in (1, 2, 3):
+        wholes.append(whole)
         mine = moved(half, *ways[level])
+        if level == 2:
+            drive, _ = lax.optimization_barrier((drive, half))
+            total = call(
+                summary_kernel, [V] * 6, V, big,
+                [pltpu.VMEM((chains, rows, grid), F32)] * 2 + [pltpu.VMEM((frames, grid), F32)],
+            )(gains, smooth_gains, transition, drive, prefix, start)
+            mine, total = lax.optimization_barrier((mine, total))
+        if level == 3:
+            total, later = call(
+                functools.partial(merged_kernel, 0), [V] * 4, [V, V], [big, big]
+            )(wholes[0], others[0], total, moved(total, *ways[0]))
+            mine, total = lax.optimization_barrier((mine, total))
         theirs = moved(mine, *ways[0])
         whole, half, other = call(
             functools.partial(halves_kernel, level), [V] * 3, [V] * 3, [big, small, big], held
         )(whole, mine, theirs)
         others.append(other)
     mine = moved(half, *ways[4])
+    if MERGED > 1:
+        total, _ = lax.optimization_barrier((total, half))
+        total, later = call(
+            functools.partial(merged_kernel, 1), [V] * 5, [V, V], [big, big]
+        )(wholes[1], others[1], total, moved(total, *ways[1]), later)
     theirs = moved(mine, *ways[0])
     end, group = call(
         functools.partial(end_kernel, 4), [V] * 3, [V, V], [shape(VEC, grid), big], held
     )(whole, mine, theirs)
     end = moved(end, *ways[5])
     starts, shifts = call(
-        starts_kernel, [V] * 6, [V, V], [shape(chains, grid, grid), shape(VEC, grid)],
+        starts_kernel, [V] * 8, [V, V], [shape(chains + 2, grid, grid), shape(VEC, grid)],
         [pltpu.VMEM((rows, grid), F32)],
-    )(*others, prefix, start)
+    )(*others, prefix, start, total, later)
 
     share = frames // parts
-    filtered, weight, value, send = call(
-        final_kernel, [V] * 8, [V] * 4,
-        [shape(share, grid)] * 3 + [shape(blocks, 2 * grid)],
+    state, send = call(
+        send_kernel, [V] * 4, [V, V], [shape(VEC, grid), shape(blocks, 1, 2 * grid)]
+    )(end, group, starts, shifts)
+    got = lax.all_to_all(send, among, 0, 0, tiled=True)[:, 0]
+    filtered, weight, value = call(
+        final_kernel, [V] * 7, [V] * 3, [shape(share, grid)] * 3,
         [pltpu.VMEM((frames, grid), F32)] * 3,
-    )(end, group, starts, shifts, drive, gains, smooth_gains, transition)
-    got = lax.all_to_all(send, TM, 0, 0, tiled=True)
+    )(state, starts, shifts, drive, gains, smooth_gains, transition)
     smoothed = call(smooth_kernel, [V, V, V], V, shape(share, grid))(
         got, weight, value
     )
@@ -333,7 +467,7 @@
 
 
 def solution(mesh):
-    torus = Mesh(mesh.devices.reshape(4, 8, 2, mesh.shape["mp"]), ("x", "z", "c", "y"))
+    torus = Mesh(mesh.devices.reshape(4, 4, 2, 2, mesh.shape["mp"]), ("x", "q", "k", "c", "y"))
     return jax.shard_map(
         on_device,
         mesh=torus,

time: 87 us -> 81.6 us (0.938)
  the two profiles are of different devices: /device:TPU:1 before, /device:TPU:8 now
where the time goes in v2:
time: 81.6 us; the launch traced here: 81.4 us
  waiting for transfers between devices  31.1 us (38%)
  starting transfers between devices  29.5 us (36%)
  Pallas kernels  20 us (25%)
    ppermute x12, waiting for transfers between devices, moved(): lax.ppermute(a, axis, [(k, to(k)) for k in range(lax.axis_size(axis))])  23 us
    ppermute x12, starting transfers between devices, moved(): lax.ppermute(a, axis, [(k, to(k)) for k in range(lax.axis_size(axis))])  15.9 us
    all_to_all x1, starting transfers between devices, on_device(): got = lax.all_to_all(send, among, 0, 0, tiled=True)[:, 0]  8.59 us
    all_to_all x1, waiting for transfers between devices, on_device(): got = lax.all_to_all(send, among, 0, 0, tiled=True)[:, 0]  8.04 us
    pallas_call x1, Pallas kernels, on_device(): call(summary_kernel, [V] * 6, V, big, [pltpu.VMEM((chains, rows, grid), F...  5.08 us
    ppermute x3, starting transfers between devices, on_device(): lax.ppermute(partial, 'y', [(k, (k + s) % parts) for k in range(parts)])  5 us
    pallas_call x1, Pallas kernels, on_device(): call(block_kernel, [V, V], [V, V], [shape(chains, grid, grid), shape(chai...  3.87 us
    pallas_call x1, Pallas kernels, on_device(): call(network_kernel, [H] * 4, V, shape(frames, grid), [pltpu.VMEM(feature...  2.85 us
  transfers between devices with their start and end apart: 16, of which 11 were waited for; matrix products, arithmetic and copies ran while one was open for 0% of the time, Pallas kernels for 16%

profile of v2, /device:TPU:8, one launch (start us, length us, event | category | flops | bytes accessed | tf_op | source)
XLA Modules:
  0.0 81.4 jit_solution(15805161011739281738)
XLA Ops:
  0.7 2.9 %shard_map.95.one_ref = f32[32,256]{1,0:T(8,128)S(1)} custom-call(bf16[32,2048]{1,0:T(8,128)(2,1)} %features_hbm.1, bf16[2048,1024]{1,0:T(8,128)(2,1)} %w_in_hbm.1, f32[1,1024]{1,0:T(1,128)} %bitcast.7, bf16[1024,256]{1,0:T(8,128)(2,1)} %out_weight_hbm.1), custom_call_target="tpu_custom_call" | custom-call | tf_op jit(solution)/shard_map/pallas_call | solution.py:381
  3.5 2.3 %collective-permute-start.2 = (f32[32,256]{1,0:T(8,128)S(1)}, f32[32,256]{1,0:T(8,128)S(1)}, u32[]{:S(2)}, u32[]{:S(2)}) collective-permute-start(f32[32,256]{1,0:T(8,128)S(1)} %shard_map.95.one_ref), channel_id=1, source_target_pairs={{0,3},{1,0},{2,1},{3,2},{4,7},{5,4},{6,5},{7,6},{8,11},{9,8},{10,9... | collective-permute-start | bytes 98312 | tf_op jit(solution)/shard_map/ppermute | solution.py:390
  5.8 0.9 %collective-permute-start.1 = (f32[32,256]{1,0:T(8,128)S(1)}, f32[32,256]{1,0:T(8,128)S(1)}, u32[]{:S(2)}, u32[]{:S(2)}) collective-permute-start(f32[32,256]{1,0:T(8,128)S(1)} %shard_map.95.one_ref), channel_id=1, source_target_pairs={{0,2},{1,3},{2,0},{3,1},{4,6},{5,7},{6,4},{7,5},{8,10},{9,11},{10,... | collective-permute-start | bytes 98312 | tf_op jit(solution)/shard_map/ppermute | solution.py:390
  6.6 1.9 %collective-permute-start = (f32[32,256]{1,0:T(8,128)S(1)}, f32[32,256]{1,0:T(8,128)S(1)}, u32[]{:S(2)}, u32[]{:S(2)}) collective-permute-start(f32[32,256]{1,0:T(8,128)S(1)} %shard_map.95.one_ref), channel_id=1, source_target_pairs={{0,1},{1,2},{2,3},{3,0},{4,5},{5,6},{6,7},{7,4},{8,9},{9,10},{10,1... | collective-permute-start | bytes 98312 | tf_op jit(solution)/shard_map/ppermute | solution.py:390
  8.5 0.0 copy-done.1
  8.5 3.9 %shard_map.96 = (f32[4,256,256]{2,1,0:T(8,128)S(1)}, f32[4,256,256]{2,1,0:T(8,128)S(1)}) custom-call(f32[32,256]{1,0:T(8,128)S(1)} %copy-done.1, f32[256,256]{1,0:T(8,128)S(1)} %copy-done), custom_call_target="tpu_custom_call" | custom-call | tf_op jit(solution)/shard_map/pallas_call | solution.py:394
  12.4 0.0 collective-permute-done.2.four_ref
  12.4 0.0 collective-permute-done.1.three_ref
  12.4 0.0 collective-permute-done.two_ref
  12.5 1.4 %shard_map.97 = (f32[264,256]{1,0:T(8,128)S(1)}, f32[32,256]{1,0:T(8,128)S(1)}, f32[8,256]{1,0:T(8,128)S(1)}) custom-call(f32[32,256]{1,0:T(8,128)S(1)} %shard_map.95.one_ref, f32[32,256]{1,0:T(8,128)S(1)} %collective-permute-done.two_ref, f32[32,256]{1,0:T(8,128)S(1)} %collective-permute-done.1.three_ref, f32[32,256]{1,0:T(8,128)S(1)} %collective-permute-done.2.four_ref, ...), custom_call_target="tpu_custom_call" | custom-call | tf_op jit(solution)/shard_map/pallas_call | solution.py:398
  13.8 0.0 collective-permute-start.3
  13.9 1.5 %collective-permute-done.3.other_ref.refs_1_.refs_0_ = f32[264,256]{1,0:T(8,128)S(1)} collective-permute-done((f32[264,256]{1,0:T(8,128)S(1)}, f32[264,256]{1,0:T(8,128)S(1)}, u32[]{:S(2)}, u32[]{:S(2)}) %collective-permute-start.3) | collective-permute-done | bytes 270368 | tf_op jit(solution)/shard_map/ppermute | solution.py:407
  15.4 0.4 shard_map.98
  15.8 2.0 %collective-permute-start.4 = (f32[136,256]{1,0:T(8,128)S(1)}, f32[136,256]{1,0:T(8,128)S(1)}, u32[]{:S(2)}, u32[]{:S(2)}) collective-permute-start(f32[136,256]{1,0:T(8,128)S(1)} %get-tuple-element.41), channel_id=1, source_target_pairs={{0,8},{8,0},{16,24},{24,16},{32,40},{40,32},{48,56},{56,48},{1,9},... | collective-permute-start | bytes 417800 | tf_op jit(solution)/shard_map/ppermute | solution.py:407
  17.8 4.0 %collective-permute-done.4.mine_ref = f32[136,256]{1,0:T(8,128)S(1)} collective-permute-done((f32[136,256]{1,0:T(8,128)S(1)}, f32[136,256]{1,0:T(8,128)S(1)}, u32[]{:S(2)}, u32[]{:S(2)}) %collective-permute-start.4) | collective-permute-done | bytes 139296 | tf_op jit(solution)/shard_map/ppermute | solution.py:407
  21.8 0.0 collective-permute-start.5
  21.8 1.4 %collective-permute-done.5.theirs_ref = f32[136,256]{1,0:T(8,128)S(1)} collective-permute-done((f32[136,256]{1,0:T(8,128)S(1)}, f32[136,256]{1,0:T(8,128)S(1)}, u32[]{:S(2)}, u32[]{:S(2)}) %collective-permute-start.5) | collective-permute-done | bytes 139296 | tf_op jit(solution)/shard_map/ppermute | solution.py:407
  23.1 0.4 shard_map.99
  23.5 3.5 %collective-permute-start.6 = (f32[136,256]{1,0:T(8,128)S(1)}, f32[136,256]{1,0:T(8,128)S(1)}, u32[]{:S(2)}, u32[]{:S(2)}) collective-permute-start(f32[136,256]{1,0:T(8,128)S(1)} %get-tuple-element.43), channel_id=1, source_target_pairs={{0,16},{8,24},{16,0},{24,8},{32,48},{40,56},{48,32},{56,40},{1,17}... | collective-permute-start | bytes 417800 | tf_op jit(solution)/shard_map/ppermute | solution.py:407
  27.1 5.1 %shard_map.100.refs_2_ = f32[264,256]{1,0:T(8,128)S(1)} custom-call(f32[32,256]{1,0:T(8,128)S(1)} %copy-done.1, f32[32,256]{1,0:T(8,128)S(1)} %copy-done.2, f32[256,256]{1,0:T(8,128)S(1)} %copy-done, f32[32,256]{1,0:T(8,128)S(1)} %get-tuple-element.45.drive_ref, f32[4,256,256]{2,1,0:T(8,128)S(1)} %get-tuple-element.38.prefix_ref.refs_4_, ...), custom_call_target="tpu_custom_call" | custom-call | tf_op jit(solution)/shard_map/pallas_call | solution.py:423
  32.2 1.9 %collective-permute-done.6.mine_ref = f32[136,256]{1,0:T(8,128)S(1)} collective-permute-done((f32[136,256]{1,0:T(8,128)S(1)}, f32[136,256]{1,0:T(8,128)S(1)}, u32[]{:S(2)}, u32[]{:S(2)}) %collective-permute-start.6) | collective-permute-done | bytes 139296 | tf_op jit(solution)/shard_map/ppermute | solution.py:407
  34.1 0.0 collective-permute-start.7
  34.1 0.5 collective-permute-start.9
  34.6 0.8 %collective-permute-done.7.theirs_ref = f32[136,256]{1,0:T(8,128)S(1)} collective-permute-done((f32[136,256]{1,0:T(8,128)S(1)}, f32[136,256]{1,0:T(8,128)S(1)}, u32[]{:S(2)}, u32[]{:S(2)}) %collective-permute-start.7) | collective-permute-done | bytes 139296 | tf_op jit(solution)/shard_map/ppermute | solution.py:407
  35.4 0.4 shard_map.101
  35.8 5.1 %collective-permute-start.8 = (f32[136,256]{1,0:T(8,128)S(1)}, f32[136,256]{1,0:T(8,128)S(1)}, u32[]{:S(2)}, u32[]{:S(2)}) collective-permute-start(f32[136,256]{1,0:T(8,128)S(1)} %get-tuple-element.49), channel_id=1, source_target_pairs={{0,56},{8,48},{16,40},{24,32},{32,24},{40,16},{48,8},{56,0},{1,57}... | collective-permute-start | bytes 417800 | tf_op jit(solution)/shard_map/ppermute | solution.py:407
  40.9 0.0 collective-permute-done.9.refs_3_
  40.9 0.3 shard_map.102
  41.2 5.7 %collective-permute-done.8.mine_ref = f32[136,256]{1,0:T(8,128)S(1)} collective-permute-done((f32[136,256]{1,0:T(8,128)S(1)}, f32[136,256]{1,0:T(8,128)S(1)}, u32[]{:S(2)}, u32[]{:S(2)}) %collective-permute-start.8) | collective-permute-done | bytes 139296 | tf_op jit(solution)/shard_map/ppermute | solution.py:407
  46.9 0.1 collective-permute-start.10
  47.0 1.3 %collective-permute-done.10.theirs_ref = f32[136,256]{1,0:T(8,128)S(1)} collective-permute-done((f32[136,256]{1,0:T(8,128)S(1)}, f32[136,256]{1,0:T(8,128)S(1)}, u32[]{:S(2)}, u32[]{:S(2)}) %collective-permute-start.10) | collective-permute-done | bytes 139296 | tf_op jit(solution)/shard_map/ppermute | solution.py:407
  48.3 0.4 shard_map.103
  48.7 1.6 %collective-permute-start.11 = (f32[136,256]{1,0:T(8,128)S(1)}, f32[136,256]{1,0:T(8,128)S(1)}, u32[]{:S(2)}, u32[]{:S(2)}) collective-permute-start(f32[136,256]{1,0:T(8,128)S(1)} %get-tuple-element.54), channel_id=1, source_target_pairs={{0,64},{64,0},{128,192},{192,128},{1,65},{65,1},{129,193},{193,129... | collective-permute-start | bytes 417800 | tf_op jit(solution)/shard_map/ppermute | solution.py:407
  50.2 0.0 collective-permute-start.14
  50.2 4.2 %collective-permute-done.11.mine_ref = f32[136,256]{1,0:T(8,128)S(1)} collective-permute-done((f32[136,256]{1,0:T(8,128)S(1)}, f32[136,256]{1,0:T(8,128)S(1)}, u32[]{:S(2)}, u32[]{:S(2)}) %collective-permute-start.11) | collective-permute-done | bytes 139296 | tf_op jit(solution)/shard_map/ppermute | solution.py:407
  54.5 0.0 collective-permute-start.12
  54.5 1.4 %collective-permute-done.12.theirs_ref = f32[136,256]{1,0:T(8,128)S(1)} collective-permute-done((f32[136,256]{1,0:T(8,128)S(1)}, f32[136,256]{1,0:T(8,128)S(1)}, u32[]{:S(2)}, u32[]{:S(2)}) %collective-permute-start.12) | collective-permute-done | bytes 139296 | tf_op jit(solution)/shard_map/ppermute | solution.py:407
  55.8 0.2 shard_map.104
  56.1 3.0 %collective-permute-start.13 = (f32[8,256]{1,0:T(8,128)S(1)}, f32[8,256]{1,0:T(8,128)S(1)}, u32[]{:S(2)}, u32[]{:S(2)}) collective-permute-start(f32[8,256]{1,0:T(8,128)S(1)} %get-tuple-element.55), channel_id=1, source_target_pairs={{0,128},{64,192},{128,0},{192,64},{1,129},{65,193},{129,1},{193,65... | collective-permute-start | bytes 24584 | tf_op jit(solution)/shard_map/ppermute | solution.py:407
  59.1 0.0 collective-permute-done.14.refs_3_
  59.1 0.3 shard_map.105
  59.4 1.0 %shard_map.106 = (f32[6,256,256]{2,1,0:T(8,128)S(1)}, f32[8,256]{1,0:T(8,128)S(1)}) custom-call(f32[264,256]{1,0:T(8,128)S(1)} %collective-permute-done.3.other_ref.refs_1_.refs_0_, f32[264,256]{1,0:T(8,128)S(1)} %get-tuple-element.57.refs_1_, f32[264,256]{1,0:T(8,128)S(1)} %get-tuple-element.58.refs_2_, f32[264,256]{1,0:T(8,128)S(1)} %get-tuple-element.59.refs_3_, ...), custom_call_target="tpu_custom_call" | custom-call | tf_op jit(solution)/shard_map/pallas_call | solution.py:449
  60.4 0.8 %collective-permute-done.13.end_ref = f32[8,256]{1,0:T(8,128)S(1)} collective-permute-done((f32[8,256]{1,0:T(8,128)S(1)}, f32[8,256]{1,0:T(8,128)S(1)}, u32[]{:S(2)}, u32[]{:S(2)}) %collective-permute-start.13) | collective-permute-done | bytes 8224 | tf_op jit(solution)/shard_map/ppermute | solution.py:407
  61.3 0.9 %shard_map.107 = (f32[8,256]{1,0:T(8,128)S(1)}, f32[16,1,512]{2,1,0:T(1,128)}) custom-call(f32[8,256]{1,0:T(8,128)S(1)} %collective-permute-done.13.end_ref, f32[264,256]{1,0:T(8,128)S(1)} %get-tuple-element.56.group_ref, f32[6,256,256]{2,1,0:T(8,128)S(1)} %get-tuple-element.65.starts_ref, f32[8,256]{1,0:T(8,128)S(1)} %get-tuple-element.66.shifts_ref), custom_call_target="tpu_custom_call" | custom-call | tf_op jit(solution)/shard_map/pallas_call | solution.py:455
  62.2 8.6 %all-to-all-start = ((f32[16,1,512]{2,1,0:T(1,128)}), f32[16,1,512]{2,1,0:T(1,128)S(1)}, u32[]{:S(2)}, u32[]{:S(2)}) async-start(f32[16,1,512]{2,1,0:T(1,128)} %get-tuple-element.69), calls=%async_computation | async-start | bytes 65536 | tf_op jit(solution)/shard_map/all_to_all | solution.py:458
  70.8 2.0 %shard_map.108 = (f32[8,256]{1,0:T(8,128)}, f32[8,256]{1,0:T(8,128)S(1)}, f32[8,256]{1,0:T(8,128)S(1)}) custom-call(f32[8,256]{1,0:T(8,128)S(1)} %get-tuple-element.67.state_ref, f32[6,256,256]{2,1,0:T(8,128)S(1)} %get-tuple-element.65.starts_ref, f32[8,256]{1,0:T(8,128)S(1)} %get-tuple-element.66.shifts_ref, f32[32,256]{1,0:T(8,128)S(1)} %get-tuple-element.45.drive_ref, ...), custom_call_target="tpu_custom_call" | custom-call | tf_op jit(solution)/shard_map/pallas_call | solution.py:459
  72.7 8.0 %all-to-all-done = f32[16,1,512]{2,1,0:T(1,128)S(1)} async-done(((f32[16,1,512]{2,1,0:T(1,128)}), f32[16,1,512]{2,1,0:T(1,128)S(1)}, u32[]{:S(2)}, u32[]{:S(2)}) %all-to-all-start) | async-done | bytes 32800 | tf_op jit(solution)/shard_map/all_to_all | solution.py:458
  80.8 0.7 shard_map.109
  (8 shorter events, 0.0 us)
Async XLA Ops:
  0.6 7.9 %copy-start.1 = (f32[32,256]{1,0:T(8,128)S(1)}, f32[32,256]{1,0:T(8,128)}, u32[]{:S(2)}) copy-start(f32[32,256]{1,0:T(8,128)} %gains_ref.7) | copy-start | bytes 98308
  0.6 7.9 %copy-start = (f32[256,256]{1,0:T(8,128)S(1)}, f32[256,256]{1,0:T(8,128)}, u32[]{:S(2)}) copy-start(f32[256,256]{1,0:T(8,128)} %transition_ref.7) | copy-start | bytes 786436
  0.7 11.8 %copy-start.3 = (f32[256]{0:T(256)S(1)}, f32[256]{0:T(256)}, u32[]{:S(2)}) copy-start(f32[256]{0:T(256)} %param.12) | copy-start | bytes 3076
  0.7 26.4 %copy-start.2 = (f32[32,256]{1,0:T(8,128)S(1)}, f32[32,256]{1,0:T(8,128)}, u32[]{:S(2)}) copy-start(f32[32,256]{1,0:T(8,128)} %smooth_ref.3) | copy-start | bytes 98308
  3.5 8.9 %collective-permute-start.2 = (f32[32,256]{1,0:T(8,128)S(1)}, f32[32,256]{1,0:T(8,128)S(1)}, u32[]{:S(2)}, u32[]{:S(2)}) collective-permute-start(f32[32,256]{1,0:T(8,128)S(1)} %shard_map.95.one_ref), channel_id=1, source_target_pairs={{0,3},{1,0},{2,1},{3,2},{4,7},{5,4},{6,5},{7,6},{8,11},{9,8},{10,9... | collective-permute-start | bytes 98312 | tf_op jit(solution)/shard_map/ppermute | solution.py:390
  5.8 6.6 %collective-permute-start.1 = (f32[32,256]{1,0:T(8,128)S(1)}, f32[32,256]{1,0:T(8,128)S(1)}, u32[]{:S(2)}, u32[]{:S(2)}) collective-permute-start(f32[32,256]{1,0:T(8,128)S(1)} %shard_map.95.one_ref), channel_id=1, source_target_pairs={{0,2},{1,3},{2,0},{3,1},{4,6},{5,7},{6,4},{7,5},{8,10},{9,11},{10,... | collective-permute-start | bytes 98312 | tf_op jit(solution)/shard_map/ppermute | solution.py:390
  6.6 5.8 %collective-permute-start = (f32[32,256]{1,0:T(8,128)S(1)}, f32[32,256]{1,0:T(8,128)S(1)}, u32[]{:S(2)}, u32[]{:S(2)}) collective-permute-start(f32[32,256]{1,0:T(8,128)S(1)} %shard_map.95.one_ref), channel_id=1, source_target_pairs={{0,1},{1,2},{2,3},{3,0},{4,5},{5,6},{6,7},{7,4},{8,9},{9,10},{10,1... | collective-permute-start | bytes 98312 | tf_op jit(solution)/shard_map/ppermute | solution.py:390
  13.8 1.6 %collective-permute-start.3 = (f32[264,256]{1,0:T(8,128)S(1)}, f32[264,256]{1,0:T(8,128)S(1)}, u32[]{:S(2)}, u32[]{:S(2)}) collective-permute-start(f32[264,256]{1,0:T(8,128)S(1)} %get-tuple-element.39.own_ref.refs_0_), channel_id=1, source_target_pairs={{0,4},{4,0},{1,5},{5,1},{2,6},{6,2},{3,7},{7,3},{8,12},{12,8},{9,1... | collective-permute-start | bytes 811016 | tf_op jit(solution)/shard_map/ppermute | solution.py:407
  15.8 6.0 %collective-permute-start.4 = (f32[136,256]{1,0:T(8,128)S(1)}, f32[136,256]{1,0:T(8,128)S(1)}, u32[]{:S(2)}, u32[]{:S(2)}) collective-permute-start(f32[136,256]{1,0:T(8,128)S(1)} %get-tuple-element.41), channel_id=1, source_target_pairs={{0,8},{8,0},{16,24},{24,16},{32,40},{40,32},{48,56},{56,48},{1,9},... | collective-permute-start | bytes 417800 | tf_op jit(solution)/shard_map/ppermute | solution.py:407
  21.8 1.4 %collective-permute-start.5 = (f32[136,256]{1,0:T(8,128)S(1)}, f32[136,256]{1,0:T(8,128)S(1)}, u32[]{:S(2)}, u32[]{:S(2)}) collective-permute-start(f32[136,256]{1,0:T(8,128)S(1)} %collective-permute-done.4.mine_ref), channel_id=1, source_target_pairs={{0,4},{4,0},{1,5},{5,1},{2,6},{6,2},{3,7},{7,3},{8,12},{12,8},{9,1... | collective-permute-start | bytes 417800 | tf_op jit(solution)/shard_map/ppermute | solution.py:407
  23.5 10.5 %collective-permute-start.6 = (f32[136,256]{1,0:T(8,128)S(1)}, f32[136,256]{1,0:T(8,128)S(1)}, u32[]{:S(2)}, u32[]{:S(2)}) collective-permute-start(f32[136,256]{1,0:T(8,128)S(1)} %get-tuple-element.43), channel_id=1, source_target_pairs={{0,16},{8,24},{16,0},{24,8},{32,48},{40,56},{48,32},{56,40},{1,17}... | collective-permute-start | bytes 417800 | tf_op jit(solution)/shard_map/ppermute | solution.py:407
  34.1 1.4 %collective-permute-start.7 = (f32[136,256]{1,0:T(8,128)S(1)}, f32[136,256]{1,0:T(8,128)S(1)}, u32[]{:S(2)}, u32[]{:S(2)}) collective-permute-start(f32[136,256]{1,0:T(8,128)S(1)} %collective-permute-done.6.mine_ref), channel_id=1, source_target_pairs={{0,4},{4,0},{1,5},{5,1},{2,6},{6,2},{3,7},{7,3},{8,12},{12,8},{9,1... | collective-permute-start | bytes 417800 | tf_op jit(solution)/shard_map/ppermute | solution.py:407
  34.1 6.9 %collective-permute-start.9 = (f32[264,256]{1,0:T(8,128)S(1)}, f32[264,256]{1,0:T(8,128)S(1)}, u32[]{:S(2)}, u32[]{:S(2)}) collective-permute-start(f32[264,256]{1,0:T(8,128)S(1)} %shard_map.100.refs_2_), channel_id=1, source_target_pairs={{0,4},{4,0},{1,5},{5,1},{2,6},{6,2},{3,7},{7,3},{8,12},{12,8},{9,1... | collective-permute-start | bytes 811016 | tf_op jit(solution)/shard_map/ppermute | solution.py:407
  35.8 11.1 %collective-permute-start.8 = (f32[136,256]{1,0:T(8,128)S(1)}, f32[136,256]{1,0:T(8,128)S(1)}, u32[]{:S(2)}, u32[]{:S(2)}) collective-permute-start(f32[136,256]{1,0:T(8,128)S(1)} %get-tuple-element.49), channel_id=1, source_target_pairs={{0,56},{8,48},{16,40},{24,32},{32,24},{40,16},{48,8},{56,0},{1,57}... | collective-permute-start | bytes 417800 | tf_op jit(solution)/shard_map/ppermute | solution.py:407
  46.9 1.4 %collective-permute-start.10 = (f32[136,256]{1,0:T(8,128)S(1)}, f32[136,256]{1,0:T(8,128)S(1)}, u32[]{:S(2)}, u32[]{:S(2)}) collective-permute-start(f32[136,256]{1,0:T(8,128)S(1)} %collective-permute-done.8.mine_ref), channel_id=1, source_target_pairs={{0,4},{4,0},{1,5},{5,1},{2,6},{6,2},{3,7},{7,3},{8,12},{12,8},{9,1... | collective-permute-start | bytes 417800 | tf_op jit(solution)/shard_map/ppermute | solution.py:407
  48.7 5.8 %collective-permute-start.11 = (f32[136,256]{1,0:T(8,128)S(1)}, f32[136,256]{1,0:T(8,128)S(1)}, u32[]{:S(2)}, u32[]{:S(2)}) collective-permute-start(f32[136,256]{1,0:T(8,128)S(1)} %get-tuple-element.54), channel_id=1, source_target_pairs={{0,64},{64,0},{128,192},{192,128},{1,65},{65,1},{129,193},{193,129... | collective-permute-start | bytes 417800 | tf_op jit(solution)/shard_map/ppermute | solution.py:407
  50.2 8.9 %collective-permute-start.14 = (f32[264,256]{1,0:T(8,128)S(1)}, f32[264,256]{1,0:T(8,128)S(1)}, u32[]{:S(2)}, u32[]{:S(2)}) collective-permute-start(f32[264,256]{1,0:T(8,128)S(1)} %get-tuple-element.61.refs_2_), channel_id=1, source_target_pairs={{0,8},{8,0},{16,24},{24,16},{32,40},{40,32},{48,56},{56,48},{1,9},... | collective-permute-start | bytes 811016 | tf_op jit(solution)/shard_map/ppermute | solution.py:407
  54.5 1.4 %collective-permute-start.12 = (f32[136,256]{1,0:T(8,128)S(1)}, f32[136,256]{1,0:T(8,128)S(1)}, u32[]{:S(2)}, u32[]{:S(2)}) collective-permute-start(f32[136,256]{1,0:T(8,128)S(1)} %collective-permute-done.11.mine_ref), channel_id=1, source_target_pairs={{0,4},{4,0},{1,5},{5,1},{2,6},{6,2},{3,7},{7,3},{8,12},{12,8},{9,1... | collective-permute-start | bytes 417800 | tf_op jit(solution)/shard_map/ppermute | solution.py:407
  56.1 5.2 %collective-permute-start.13 = (f32[8,256]{1,0:T(8,128)S(1)}, f32[8,256]{1,0:T(8,128)S(1)}, u32[]{:S(2)}, u32[]{:S(2)}) collective-permute-start(f32[8,256]{1,0:T(8,128)S(1)} %get-tuple-element.55), channel_id=1, source_target_pairs={{0,128},{64,192},{128,0},{192,64},{1,129},{65,193},{129,1},{193,65... | collective-permute-start | bytes 24584 | tf_op jit(solution)/shard_map/ppermute | solution.py:407
  62.2 18.6 %all-to-all-start = ((f32[16,1,512]{2,1,0:T(1,128)}), f32[16,1,512]{2,1,0:T(1,128)S(1)}, u32[]{:S(2)}, u32[]{:S(2)}) async-start(f32[16,1,512]{2,1,0:T(1,128)} %get-tuple-element.69), calls=%async_computation | async-start | bytes 65536 | tf_op jit(solution)/shard_map/all_to_all | solution.py:458

commit v3 on v2

--- a/solution.py
+++ b/solution.py
@@ -407,8 +407,8 @@
         return lax.ppermute(a, axis, [(k, to(k)) for k in range(lax.axis_size(axis))])
 
     ways = [
-        ("c", lambda k: 1 - k), (Z, lambda k: k ^ 1), (Z, lambda k: k ^ 2),
-        (Z, lambda k: 7 - k), ("x", lambda k: k ^ 1), ("x", lambda k: k ^ 2),
+        ("c", lambda k: 1 - k), (Z, lambda k: k ^ 1), (Z, lambda k: k ^ 3),
+        (Z, lambda k: 7 - k), ("x", lambda k: k ^ 1), ("x", lambda k: 3 - k),
     ]
     wholes = [whole]
     others = [moved(whole, *ways[0])]

time: 81.6 us -> 79.6 us (0.975)
  the two profiles are of different devices: /device:TPU:8 before, /device:TPU:1 now
where the time goes in v3:
time: 79.6 us; the launch traced here: 78 us
  starting transfers between devices  31 us (39%)
  waiting for transfers between devices  25.8 us (32%)
  Pallas kernels  20.4 us (26%)
    ppermute x12, starting transfers between devices, moved(): lax.ppermute(a, axis, [(k, to(k)) for k in range(lax.axis_size(axis))])  19.1 us
    ppermute x12, waiting for transfers between devices, moved(): lax.ppermute(a, axis, [(k, to(k)) for k in range(lax.axis_size(axis))])  18.8 us
    all_to_all x1, starting transfers between devices, on_device(): got = lax.all_to_all(send, among, 0, 0, tiled=True)[:, 0]  7.24 us
    all_to_all x1, waiting for transfers between devices, on_device(): got = lax.all_to_all(send, among, 0, 0, tiled=True)[:, 0]  6.98 us
    pallas_call x1, Pallas kernels, on_device(): call(summary_kernel, [V] * 6, V, big, [pltpu.VMEM((chains, rows, grid), F...  5.08 us
    ppermute x3, starting transfers between devices, on_device(): lax.ppermute(partial, 'y', [(k, (k + s) % parts) for k in range(parts)])  4.68 us
    pallas_call x1, Pallas kernels, on_device(): call(block_kernel, [V, V], [V, V], [shape(chains, grid, grid), shape(chai...  3.87 us
    pallas_call x1, Pallas kernels, on_device(): call(network_kernel, [H] * 4, V, shape(frames, grid), [pltpu.VMEM(feature...  2.85 us
  transfers between devices with their start and end apart: 16, of which 9 were waited for; matrix products, arithmetic and copies ran while one was open for 0% of the time, Pallas kernels for 17%

profile of v3, /device:TPU:1, one launch (start us, length us, event | category | flops | bytes accessed | tf_op | source)
XLA Modules:
  0.0 78.0 jit_solution(6714525726483874972)
XLA Ops:
  0.7 2.9 %shard_map.95.one_ref = f32[32,256]{1,0:T(8,128)S(1)} custom-call(bf16[32,2048]{1,0:T(8,128)(2,1)} %features_hbm.1, bf16[2048,1024]{1,0:T(8,128)(2,1)} %w_in_hbm.1, f32[1,1024]{1,0:T(1,128)} %bitcast.7, bf16[1024,256]{1,0:T(8,128)(2,1)} %out_weight_hbm.1), custom_call_target="tpu_custom_call" | custom-call | tf_op jit(solution)/shard_map/pallas_call | solution.py:381
  3.5 3.6 %collective-permute-start.2 = (f32[32,256]{1,0:T(8,128)S(1)}, f32[32,256]{1,0:T(8,128)S(1)}, u32[]{:S(2)}, u32[]{:S(2)}) collective-permute-start(f32[32,256]{1,0:T(8,128)S(1)} %shard_map.95.one_ref), channel_id=1, source_target_pairs={{0,3},{1,0},{2,1},{3,2},{4,7},{5,4},{6,5},{7,6},{8,11},{9,8},{10,9... | collective-permute-start | bytes 98312 | tf_op jit(solution)/shard_map/ppermute | solution.py:390
  7.2 0.3 collective-permute-start.1
  7.5 0.7 collective-permute-start
  8.2 0.0 copy-done.1
  8.2 3.9 %shard_map.96 = (f32[4,256,256]{2,1,0:T(8,128)S(1)}, f32[4,256,256]{2,1,0:T(8,128)S(1)}) custom-call(f32[32,256]{1,0:T(8,128)S(1)} %copy-done.1, f32[256,256]{1,0:T(8,128)S(1)} %copy-done), custom_call_target="tpu_custom_call" | custom-call | tf_op jit(solution)/shard_map/pallas_call | solution.py:394
  12.1 0.0 collective-permute-done.2.four_ref
  12.1 0.0 collective-permute-done.1.three_ref
  12.1 0.0 collective-permute-done.two_ref
  12.1 1.4 %shard_map.97 = (f32[264,256]{1,0:T(8,128)S(1)}, f32[32,256]{1,0:T(8,128)S(1)}, f32[8,256]{1,0:T(8,128)S(1)}) custom-call(f32[32,256]{1,0:T(8,128)S(1)} %shard_map.95.one_ref, f32[32,256]{1,0:T(8,128)S(1)} %collective-permute-done.two_ref, f32[32,256]{1,0:T(8,128)S(1)} %collective-permute-done.1.three_ref, f32[32,256]{1,0:T(8,128)S(1)} %collective-permute-done.2.four_ref, ...), custom_call_target="tpu_custom_call" | custom-call | tf_op jit(solution)/shard_map/pallas_call | solution.py:398
  13.5 1.8 %collective-permute-start.3 = (f32[264,256]{1,0:T(8,128)S(1)}, f32[264,256]{1,0:T(8,128)S(1)}, u32[]{:S(2)}, u32[]{:S(2)}) collective-permute-start(f32[264,256]{1,0:T(8,128)S(1)} %get-tuple-element.39.own_ref.refs_0_), channel_id=1, source_target_pairs={{0,4},{4,0},{1,5},{5,1},{2,6},{6,2},{3,7},{7,3},{8,12},{12,8},{9,1... | collective-permute-start | bytes 811016 | tf_op jit(solution)/shard_map/ppermute | solution.py:407
  15.3 1.2 %collective-permute-done.3.other_ref.refs_1_.refs_0_ = f32[264,256]{1,0:T(8,128)S(1)} collective-permute-done((f32[264,256]{1,0:T(8,128)S(1)}, f32[264,256]{1,0:T(8,128)S(1)}, u32[]{:S(2)}, u32[]{:S(2)}) %collective-permute-start.3) | collective-permute-done | bytes 270368 | tf_op jit(solution)/shard_map/ppermute | solution.py:407
  16.5 0.4 shard_map.98
  16.9 1.7 %collective-permute-start.4 = (f32[136,256]{1,0:T(8,128)S(1)}, f32[136,256]{1,0:T(8,128)S(1)}, u32[]{:S(2)}, u32[]{:S(2)}) collective-permute-start(f32[136,256]{1,0:T(8,128)S(1)} %get-tuple-element.41), channel_id=1, source_target_pairs={{0,8},{8,0},{16,24},{24,16},{32,40},{40,32},{48,56},{56,48},{1,9},... | collective-permute-start | bytes 417800 | tf_op jit(solution)/shard_map/ppermute | solution.py:407
  18.6 3.6 %collective-permute-done.4.mine_ref = f32[136,256]{1,0:T(8,128)S(1)} collective-permute-done((f32[136,256]{1,0:T(8,128)S(1)}, f32[136,256]{1,0:T(8,128)S(1)}, u32[]{:S(2)}, u32[]{:S(2)}) %collective-permute-start.4) | collective-permute-done | bytes 139296 | tf_op jit(solution)/shard_map/ppermute | solution.py:407
  22.2 1.0 %collective-permute-start.5 = (f32[136,256]{1,0:T(8,128)S(1)}, f32[136,256]{1,0:T(8,128)S(1)}, u32[]{:S(2)}, u32[]{:S(2)}) collective-permute-start(f32[136,256]{1,0:T(8,128)S(1)} %collective-permute-done.4.mine_ref), channel_id=1, source_target_pairs={{0,4},{4,0},{1,5},{5,1},{2,6},{6,2},{3,7},{7,3},{8,12},{12,8},{9,1... | collective-permute-start | bytes 417800 | tf_op jit(solution)/shard_map/ppermute | solution.py:407
  23.2 1.0 %collective-permute-done.5.theirs_ref = f32[136,256]{1,0:T(8,128)S(1)} collective-permute-done((f32[136,256]{1,0:T(8,128)S(1)}, f32[136,256]{1,0:T(8,128)S(1)}, u32[]{:S(2)}, u32[]{:S(2)}) %collective-permute-start.5) | collective-permute-done | bytes 139296 | tf_op jit(solution)/shard_map/ppermute | solution.py:407
  24.2 0.4 shard_map.99
  24.6 4.4 %collective-permute-start.6 = (f32[136,256]{1,0:T(8,128)S(1)}, f32[136,256]{1,0:T(8,128)S(1)}, u32[]{:S(2)}, u32[]{:S(2)}) collective-permute-start(f32[136,256]{1,0:T(8,128)S(1)} %get-tuple-element.43), channel_id=1, source_target_pairs={{0,24},{8,16},{16,8},{24,0},{32,56},{40,48},{48,40},{56,32},{1,25}... | collective-permute-start | bytes 417800 | tf_op jit(solution)/shard_map/ppermute | solution.py:407
  29.1 5.1 %shard_map.100.refs_2_ = f32[264,256]{1,0:T(8,128)S(1)} custom-call(f32[32,256]{1,0:T(8,128)S(1)} %copy-done.1, f32[32,256]{1,0:T(8,128)S(1)} %copy-done.2, f32[256,256]{1,0:T(8,128)S(1)} %copy-done, f32[32,256]{1,0:T(8,128)S(1)} %get-tuple-element.45.drive_ref, f32[4,256,256]{2,1,0:T(8,128)S(1)} %get-tuple-element.38.prefix_ref.refs_4_, ...), custom_call_target="tpu_custom_call" | custom-call | tf_op jit(solution)/shard_map/pallas_call | solution.py:423
  34.1 0.0 collective-permute-done.6.mine_ref
  34.2 0.7 collective-permute-start.7
  34.9 0.1 collective-permute-start.9
  35.0 0.9 %collective-permute-done.7.theirs_ref = f32[136,256]{1,0:T(8,128)S(1)} collective-permute-done((f32[136,256]{1,0:T(8,128)S(1)}, f32[136,256]{1,0:T(8,128)S(1)}, u32[]{:S(2)}, u32[]{:S(2)}) %collective-permute-start.7) | collective-permute-done | bytes 139296 | tf_op jit(solution)/shard_map/ppermute | solution.py:407
  35.9 0.4 shard_map.101
  36.3 3.5 %collective-permute-start.8 = (f32[136,256]{1,0:T(8,128)S(1)}, f32[136,256]{1,0:T(8,128)S(1)}, u32[]{:S(2)}, u32[]{:S(2)}) collective-permute-start(f32[136,256]{1,0:T(8,128)S(1)} %get-tuple-element.49), channel_id=1, source_target_pairs={{0,56},{8,48},{16,40},{24,32},{32,24},{40,16},{48,8},{56,0},{1,57}... | collective-permute-start | bytes 417800 | tf_op jit(solution)/shard_map/ppermute | solution.py:407
  39.8 0.0 collective-permute-done.9.refs_3_
  39.8 0.3 shard_map.102
  40.1 6.4 %collective-permute-done.8.mine_ref = f32[136,256]{1,0:T(8,128)S(1)} collective-permute-done((f32[136,256]{1,0:T(8,128)S(1)}, f32[136,256]{1,0:T(8,128)S(1)}, u32[]{:S(2)}, u32[]{:S(2)}) %collective-permute-start.8) | collective-permute-done | bytes 139296 | tf_op jit(solution)/shard_map/ppermute | solution.py:407
  46.5 0.9 %collective-permute-start.10 = (f32[136,256]{1,0:T(8,128)S(1)}, f32[136,256]{1,0:T(8,128)S(1)}, u32[]{:S(2)}, u32[]{:S(2)}) collective-permute-start(f32[136,256]{1,0:T(8,128)S(1)} %collective-permute-done.8.mine_ref), channel_id=1, source_target_pairs={{0,4},{4,0},{1,5},{5,1},{2,6},{6,2},{3,7},{7,3},{8,12},{12,8},{9,1... | collective-permute-start | bytes 417800 | tf_op jit(solution)/shard_map/ppermute | solution.py:407
  47.4 1.0 %collective-permute-done.10.theirs_ref = f32[136,256]{1,0:T(8,128)S(1)} collective-permute-done((f32[136,256]{1,0:T(8,128)S(1)}, f32[136,256]{1,0:T(8,128)S(1)}, u32[]{:S(2)}, u32[]{:S(2)}) %collective-permute-start.10) | collective-permute-done | bytes 139296 | tf_op jit(solution)/shard_map/ppermute | solution.py:407
  48.4 0.4 shard_map.103
  48.8 1.3 %collective-permute-start.11 = (f32[136,256]{1,0:T(8,128)S(1)}, f32[136,256]{1,0:T(8,128)S(1)}, u32[]{:S(2)}, u32[]{:S(2)}) collective-permute-start(f32[136,256]{1,0:T(8,128)S(1)} %get-tuple-element.54), channel_id=1, source_target_pairs={{0,64},{64,0},{128,192},{192,128},{1,65},{65,1},{129,193},{193,129... | collective-permute-start | bytes 417800 | tf_op jit(solution)/shard_map/ppermute | solution.py:407
  50.1 0.0 collective-permute-start.14
  50.1 3.7 %collective-permute-done.11.mine_ref = f32[136,256]{1,0:T(8,128)S(1)} collective-permute-done((f32[136,256]{1,0:T(8,128)S(1)}, f32[136,256]{1,0:T(8,128)S(1)}, u32[]{:S(2)}, u32[]{:S(2)}) %collective-permute-start.11) | collective-permute-done | bytes 139296 | tf_op jit(solution)/shard_map/ppermute | solution.py:407
  53.8 1.2 %collective-permute-start.12 = (f32[136,256]{1,0:T(8,128)S(1)}, f32[136,256]{1,0:T(8,128)S(1)}, u32[]{:S(2)}, u32[]{:S(2)}) collective-permute-start(f32[136,256]{1,0:T(8,128)S(1)} %collective-permute-done.11.mine_ref), channel_id=1, source_target_pairs={{0,4},{4,0},{1,5},{5,1},{2,6},{6,2},{3,7},{7,3},{8,12},{12,8},{9,1... | collective-permute-start | bytes 417800 | tf_op jit(solution)/shard_map/ppermute | solution.py:407
  55.0 1.0 %collective-permute-done.12.theirs_ref = f32[136,256]{1,0:T(8,128)S(1)} collective-permute-done((f32[136,256]{1,0:T(8,128)S(1)}, f32[136,256]{1,0:T(8,128)S(1)}, u32[]{:S(2)}, u32[]{:S(2)}) %collective-permute-start.12) | collective-permute-done | bytes 139296 | tf_op jit(solution)/shard_map/ppermute | solution.py:407
  56.0 0.2 shard_map.104
  56.2 2.5 %collective-permute-start.13 = (f32[8,256]{1,0:T(8,128)S(1)}, f32[8,256]{1,0:T(8,128)S(1)}, u32[]{:S(2)}, u32[]{:S(2)}) collective-permute-start(f32[8,256]{1,0:T(8,128)S(1)} %get-tuple-element.55), channel_id=1, source_target_pairs={{0,192},{64,128},{128,64},{192,0},{1,193},{65,129},{129,65},{193,1... | collective-permute-start | bytes 24584 | tf_op jit(solution)/shard_map/ppermute | solution.py:407
  58.7 0.0 collective-permute-done.14.refs_3_
  58.7 0.3 shard_map.105
  59.0 1.3 %shard_map.106 = (f32[6,256,256]{2,1,0:T(8,128)S(1)}, f32[8,256]{1,0:T(8,128)S(1)}) custom-call(f32[264,256]{1,0:T(8,128)S(1)} %collective-permute-done.3.other_ref.refs_1_.refs_0_, f32[264,256]{1,0:T(8,128)S(1)} %get-tuple-element.57.refs_1_, f32[264,256]{1,0:T(8,128)S(1)} %get-tuple-element.58.refs_2_, f32[264,256]{1,0:T(8,128)S(1)} %get-tuple-element.59.refs_3_, ...), custom_call_target="tpu_custom_call" | custom-call | tf_op jit(solution)/shard_map/pallas_call | solution.py:449
  60.3 0.0 collective-permute-done.13.end_ref
  60.3 0.9 %shard_map.107 = (f32[8,256]{1,0:T(8,128)S(1)}, f32[16,1,512]{2,1,0:T(1,128)}) custom-call(f32[8,256]{1,0:T(8,128)S(1)} %collective-permute-done.13.end_ref, f32[264,256]{1,0:T(8,128)S(1)} %get-tuple-element.56.group_ref, f32[6,256,256]{2,1,0:T(8,128)S(1)} %get-tuple-element.65.starts_ref, f32[8,256]{1,0:T(8,128)S(1)} %get-tuple-element.66.shifts_ref), custom_call_target="tpu_custom_call" | custom-call | tf_op jit(solution)/shard_map/pallas_call | solution.py:455
  61.2 7.2 %all-to-all-start = ((f32[16,1,512]{2,1,0:T(1,128)}), f32[16,1,512]{2,1,0:T(1,128)S(1)}, u32[]{:S(2)}, u32[]{:S(2)}) async-start(f32[16,1,512]{2,1,0:T(1,128)} %get-tuple-element.69), calls=%async_computation | async-start | bytes 65536 | tf_op jit(solution)/shard_map/all_to_all | solution.py:458
  68.4 2.0 %shard_map.108 = (f32[8,256]{1,0:T(8,128)}, f32[8,256]{1,0:T(8,128)S(1)}, f32[8,256]{1,0:T(8,128)S(1)}) custom-call(f32[8,256]{1,0:T(8,128)S(1)} %get-tuple-element.67.state_ref, f32[6,256,256]{2,1,0:T(8,128)S(1)} %get-tuple-element.65.starts_ref, f32[8,256]{1,0:T(8,128)S(1)} %get-tuple-element.66.shifts_ref, f32[32,256]{1,0:T(8,128)S(1)} %get-tuple-element.45.drive_ref, ...), custom_call_target="tpu_custom_call" | custom-call | tf_op jit(solution)/shard_map/pallas_call | solution.py:459
  70.4 7.0 %all-to-all-done = f32[16,1,512]{2,1,0:T(1,128)S(1)} async-done(((f32[16,1,512]{2,1,0:T(1,128)}), f32[16,1,512]{2,1,0:T(1,128)S(1)}, u32[]{:S(2)}, u32[]{:S(2)}) %all-to-all-start) | async-done | bytes 32800 | tf_op jit(solution)/shard_map/all_to_all | solution.py:458
  77.4 0.7 shard_map.109
  (8 shorter events, 0.0 us)
Async XLA Ops:
  0.6 7.6 %copy-start.1 = (f32[32,256]{1,0:T(8,128)S(1)}, f32[32,256]{1,0:T(8,128)}, u32[]{:S(2)}) copy-start(f32[32,256]{1,0:T(8,128)} %gains_ref.7) | copy-start | bytes 98308
  0.6 7.6 %copy-start = (f32[256,256]{1,0:T(8,128)S(1)}, f32[256,256]{1,0:T(8,128)}, u32[]{:S(2)}) copy-start(f32[256,256]{1,0:T(8,128)} %transition_ref.7) | copy-start | bytes 786436
  0.7 11.5 %copy-start.3 = (f32[256]{0:T(256)S(1)}, f32[256]{0:T(256)}, u32[]{:S(2)}) copy-start(f32[256]{0:T(256)} %param.12) | copy-start | bytes 3076
  0.7 28.4 %copy-start.2 = (f32[32,256]{1,0:T(8,128)S(1)}, f32[32,256]{1,0:T(8,128)}, u32[]{:S(2)}) copy-start(f32[32,256]{1,0:T(8,128)} %smooth_ref.3) | copy-start | bytes 98308
  3.5 8.6 %collective-permute-start.2 = (f32[32,256]{1,0:T(8,128)S(1)}, f32[32,256]{1,0:T(8,128)S(1)}, u32[]{:S(2)}, u32[]{:S(2)}) collective-permute-start(f32[32,256]{1,0:T(8,128)S(1)} %shard_map.95.one_ref), channel_id=1, source_target_pairs={{0,3},{1,0},{2,1},{3,2},{4,7},{5,4},{6,5},{7,6},{8,11},{9,8},{10,9... | collective-permute-start | bytes 98312 | tf_op jit(solution)/shard_map/ppermute | solution.py:390
  7.2 4.9 %collective-permute-start.1 = (f32[32,256]{1,0:T(8,128)S(1)}, f32[32,256]{1,0:T(8,128)S(1)}, u32[]{:S(2)}, u32[]{:S(2)}) collective-permute-start(f32[32,256]{1,0:T(8,128)S(1)} %shard_map.95.one_ref), channel_id=1, source_target_pairs={{0,2},{1,3},{2,0},{3,1},{4,6},{5,7},{6,4},{7,5},{8,10},{9,11},{10,... | collective-permute-start | bytes 98312 | tf_op jit(solution)/shard_map/ppermute | solution.py:390
  7.5 4.6 %collective-permute-start = (f32[32,256]{1,0:T(8,128)S(1)}, f32[32,256]{1,0:T(8,128)S(1)}, u32[]{:S(2)}, u32[]{:S(2)}) collective-permute-start(f32[32,256]{1,0:T(8,128)S(1)} %shard_map.95.one_ref), channel_id=1, source_target_pairs={{0,1},{1,2},{2,3},{3,0},{4,5},{5,6},{6,7},{7,4},{8,9},{9,10},{10,1... | collective-permute-start | bytes 98312 | tf_op jit(solution)/shard_map/ppermute | solution.py:390
  13.5 3.0 %collective-permute-start.3 = (f32[264,256]{1,0:T(8,128)S(1)}, f32[264,256]{1,0:T(8,128)S(1)}, u32[]{:S(2)}, u32[]{:S(2)}) collective-permute-start(f32[264,256]{1,0:T(8,128)S(1)} %get-tuple-element.39.own_ref.refs_0_), channel_id=1, source_target_pairs={{0,4},{4,0},{1,5},{5,1},{2,6},{6,2},{3,7},{7,3},{8,12},{12,8},{9,1... | collective-permute-start | bytes 811016 | tf_op jit(solution)/shard_map/ppermute | solution.py:407
  16.9 5.4 %collective-permute-start.4 = (f32[136,256]{1,0:T(8,128)S(1)}, f32[136,256]{1,0:T(8,128)S(1)}, u32[]{:S(2)}, u32[]{:S(2)}) collective-permute-start(f32[136,256]{1,0:T(8,128)S(1)} %get-tuple-element.41), channel_id=1, source_target_pairs={{0,8},{8,0},{16,24},{24,16},{32,40},{40,32},{48,56},{56,48},{1,9},... | collective-permute-start | bytes 417800 | tf_op jit(solution)/shard_map/ppermute | solution.py:407
  22.2 2.0 %collective-permute-start.5 = (f32[136,256]{1,0:T(8,128)S(1)}, f32[136,256]{1,0:T(8,128)S(1)}, u32[]{:S(2)}, u32[]{:S(2)}) collective-permute-start(f32[136,256]{1,0:T(8,128)S(1)} %collective-permute-done.4.mine_ref), channel_id=1, source_target_pairs={{0,4},{4,0},{1,5},{5,1},{2,6},{6,2},{3,7},{7,3},{8,12},{12,8},{9,1... | collective-permute-start | bytes 417800 | tf_op jit(solution)/shard_map/ppermute | solution.py:407
  24.6 9.5 %collective-permute-start.6 = (f32[136,256]{1,0:T(8,128)S(1)}, f32[136,256]{1,0:T(8,128)S(1)}, u32[]{:S(2)}, u32[]{:S(2)}) collective-permute-start(f32[136,256]{1,0:T(8,128)S(1)} %get-tuple-element.43), channel_id=1, source_target_pairs={{0,24},{8,16},{16,8},{24,0},{32,56},{40,48},{48,40},{56,32},{1,25}... | collective-permute-start | bytes 417800 | tf_op jit(solution)/shard_map/ppermute | solution.py:407
  34.2 1.7 %collective-permute-start.7 = (f32[136,256]{1,0:T(8,128)S(1)}, f32[136,256]{1,0:T(8,128)S(1)}, u32[]{:S(2)}, u32[]{:S(2)}) collective-permute-start(f32[136,256]{1,0:T(8,128)S(1)} %collective-permute-done.6.mine_ref), channel_id=1, source_target_pairs={{0,4},{4,0},{1,5},{5,1},{2,6},{6,2},{3,7},{7,3},{8,12},{12,8},{9,1... | collective-permute-start | bytes 417800 | tf_op jit(solution)/shard_map/ppermute | solution.py:407
  34.9 4.9 %collective-permute-start.9 = (f32[264,256]{1,0:T(8,128)S(1)}, f32[264,256]{1,0:T(8,128)S(1)}, u32[]{:S(2)}, u32[]{:S(2)}) collective-permute-start(f32[264,256]{1,0:T(8,128)S(1)} %shard_map.100.refs_2_), channel_id=1, source_target_pairs={{0,4},{4,0},{1,5},{5,1},{2,6},{6,2},{3,7},{7,3},{8,12},{12,8},{9,1... | collective-permute-start | bytes 811016 | tf_op jit(solution)/shard_map/ppermute | solution.py:407
  36.3 10.2 %collective-permute-start.8 = (f32[136,256]{1,0:T(8,128)S(1)}, f32[136,256]{1,0:T(8,128)S(1)}, u32[]{:S(2)}, u32[]{:S(2)}) collective-permute-start(f32[136,256]{1,0:T(8,128)S(1)} %get-tuple-element.49), channel_id=1, source_target_pairs={{0,56},{8,48},{16,40},{24,32},{32,24},{40,16},{48,8},{56,0},{1,57}... | collective-permute-start | bytes 417800 | tf_op jit(solution)/shard_map/ppermute | solution.py:407
  46.5 1.9 %collective-permute-start.10 = (f32[136,256]{1,0:T(8,128)S(1)}, f32[136,256]{1,0:T(8,128)S(1)}, u32[]{:S(2)}, u32[]{:S(2)}) collective-permute-start(f32[136,256]{1,0:T(8,128)S(1)} %collective-permute-done.8.mine_ref), channel_id=1, source_target_pairs={{0,4},{4,0},{1,5},{5,1},{2,6},{6,2},{3,7},{7,3},{8,12},{12,8},{9,1... | collective-permute-start | bytes 417800 | tf_op jit(solution)/shard_map/ppermute | solution.py:407
  48.8 5.0 %collective-permute-start.11 = (f32[136,256]{1,0:T(8,128)S(1)}, f32[136,256]{1,0:T(8,128)S(1)}, u32[]{:S(2)}, u32[]{:S(2)}) collective-permute-start(f32[136,256]{1,0:T(8,128)S(1)} %get-tuple-element.54), channel_id=1, source_target_pairs={{0,64},{64,0},{128,192},{192,128},{1,65},{65,1},{129,193},{193,129... | collective-permute-start | bytes 417800 | tf_op jit(solution)/shard_map/ppermute | solution.py:407
  50.1 8.6 %collective-permute-start.14 = (f32[264,256]{1,0:T(8,128)S(1)}, f32[264,256]{1,0:T(8,128)S(1)}, u32[]{:S(2)}, u32[]{:S(2)}) collective-permute-start(f32[264,256]{1,0:T(8,128)S(1)} %get-tuple-element.61.refs_2_), channel_id=1, source_target_pairs={{0,8},{8,0},{16,24},{24,16},{32,40},{40,32},{48,56},{56,48},{1,9},... | collective-permute-start | bytes 811016 | tf_op jit(solution)/shard_map/ppermute | solution.py:407
  53.8 2.2 %collective-permute-start.12 = (f32[136,256]{1,0:T(8,128)S(1)}, f32[136,256]{1,0:T(8,128)S(1)}, u32[]{:S(2)}, u32[]{:S(2)}) collective-permute-start(f32[136,256]{1,0:T(8,128)S(1)} %collective-permute-done.11.mine_ref), channel_id=1, source_target_pairs={{0,4},{4,0},{1,5},{5,1},{2,6},{6,2},{3,7},{7,3},{8,12},{12,8},{9,1... | collective-permute-start | bytes 417800 | tf_op jit(solution)/shard_map/ppermute | solution.py:407
  56.2 4.1 %collective-permute-start.13 = (f32[8,256]{1,0:T(8,128)S(1)}, f32[8,256]{1,0:T(8,128)S(1)}, u32[]{:S(2)}, u32[]{:S(2)}) collective-permute-start(f32[8,256]{1,0:T(8,128)S(1)} %get-tuple-element.55), channel_id=1, source_target_pairs={{0,192},{64,128},{128,64},{192,0},{1,193},{65,129},{129,65},{193,1... | collective-permute-start | bytes 24584 | tf_op jit(solution)/shard_map/ppermute | solution.py:407
  61.2 16.2 %all-to-all-start = ((f32[16,1,512]{2,1,0:T(1,128)}), f32[16,1,512]{2,1,0:T(1,128)S(1)}, u32[]{:S(2)}, u32[]{:S(2)}) async-start(f32[16,1,512]{2,1,0:T(1,128)} %get-tuple-element.69), calls=%async_computation | async-start | bytes 65536 | tf_op jit(solution)/shard_map/all_to_all | solution.py:458

commit v4 on v3

--- a/solution.py
+++ b/solution.py
@@ -12,6 +12,7 @@
 TM = ("x", "q", "k", "c")
 F32, BF16 = jnp.float32, jnp.bfloat16
 SUB = 8
+EARLY = 4
 MERGED = 2
 VEC = 8
 
@@ -48,15 +49,18 @@
 
 
 def network_kernel(
-    features_hbm, w_in_hbm, b_in_hbm, out_weight_hbm, partial_ref,
-    features_ref, w_in_ref, b_in_ref, out_weight_ref, pre_ref, done,
+    features_hbm, w_in_hbm, b_in_hbm, out_weight_hbm, gains_hbm, transition_hbm,
+    partial_ref, chain_ref,
+    features_ref, w_in_ref, b_in_ref, out_weight_ref, gains_ref, transition_ref, pre_ref, done,
 ):
-    pieces_in = done.shape[0] - 3
+    pieces_in = done.shape[0] - 5
     deep = w_in_ref.shape[0] // pieces_in
     small = [
         pltpu.make_async_copy(features_hbm, features_ref, done.at[pieces_in]),
         pltpu.make_async_copy(b_in_hbm, b_in_ref, done.at[pieces_in + 1]),
         pltpu.make_async_copy(out_weight_hbm, out_weight_ref, done.at[pieces_in + 2]),
+        pltpu.make_async_copy(gains_hbm, gains_ref, done.at[pieces_in + 3]),
+        pltpu.make_async_copy(transition_hbm, transition_ref, done.at[pieces_in + 4]),
     ]
     parts = [
         pltpu.make_async_copy(
@@ -64,8 +68,14 @@
         )
         for k in range(pieces_in)
     ]
-    for copy in (small[0], *parts, *small[1:]):
+    for copy in (small[4], small[3], small[0], *parts, *small[1:3]):
         copy.start()
+    small[4].wait()
+    small[3].wait()
+    flipped = transition_ref[...].T
+    for j in range(chain_ref.shape[0]):
+        chain_ref[j] = flipped * (1.0 - gains_ref[SUB * j : SUB * j + 1, :])
+    walked(chain_ref, gains_ref, right(flipped), 1, EARLY)
     small[0].wait()
     for k, copy in enumerate(parts):
         copy.wait()
@@ -78,14 +88,9 @@
     partial_ref[...] = jnp.dot(hidden, out_weight_ref[...], preferred_element_type=F32)
 
 
-def block_kernel(gains_ref, transition_ref, chain_ref, prefix_ref):
-    grid = transition_ref.shape[0]
-    chains = chain_ref.shape[0]
-    flipped = transition_ref[...].T
-    step = right(flipped)
-    for j in range(chains):
-        chain_ref[j] = flipped * (1.0 - gains_ref[SUB * j : SUB * j + 1, :])
-    for t in range(1, SUB):
+def walked(chain_ref, gains_ref, step, first, last):
+    chains, grid = chain_ref.shape[0], chain_ref.shape[1]
+    for t in range(first, last):
         for part in range(2):
             own = range(part * chains // 2, (part + 1) * chains // 2)
             moved = times(jnp.concatenate([chain_ref[j] for j in own], axis=0), step)
@@ -93,14 +98,21 @@
                 row = SUB * j + t
                 keep = 1.0 - gains_ref[row : row + 1, :]
                 chain_ref[j] = moved[n * grid : (n + 1) * grid] * keep
+
+
+def block_kernel(gains_ref, transition_ref, early_ref, whole_ref, chain_ref, prefix_ref):
+    chains = chain_ref.shape[0]
+    chain_ref[...] = early_ref[...]
+    walked(chain_ref, gains_ref, right(transition_ref[...].T), EARLY, SUB)
     prefix_ref[0] = chain_ref[0]
     for j in range(1, chains):
         prefix_ref[j] = times(prefix_ref[j - 1], right(chain_ref[j]))
+    whole_ref[...] = prefix_ref[chains - 1]
 
 
 def response_kernel(
-    one_ref, two_ref, three_ref, four_ref, offset_ref, gains_ref, transition_ref, chain_ref, prefix_ref,
-    whole_ref, drive_ref, start_ref,
+    one_ref, two_ref, three_ref, four_ref, offset_ref, gains_ref, transition_ref, chain_ref,
+    ended_ref, drive_ref, start_ref,
 ):
     chains, grid = chain_ref.shape[0], transition_ref.shape[0]
     step = right(transition_ref[...].T)
@@ -115,8 +127,7 @@
     for j in range(1, chains):
         start_ref[j : j + 1, :] = carried
         carried = times(carried, right(chain_ref[j])) + state[j : j + 1]
-    whole_ref[0:grid, :] = prefix_ref[chains - 1]
-    whole_ref[grid:, :] = jnp.concatenate([carried, jnp.zeros((VEC - 1, grid), F32)], axis=0)
+    ended_ref[...] = padded(carried)
 
 
 def after(earlier, later):
@@ -233,8 +244,15 @@
     half_ref[half:, :] = whole_ref[2 * half :, :]
 
 
-def whole_kernel(level, own_ref, other_ref, whole_ref, half_ref, held):
-    whole_ref[...] = ordered(held, own_ref[...], other_ref[...], bit(level))
+def core_kernel(
+    own_ref, other_ref, own_v_ref, other_v_ref, one_ref, two_ref, whole_ref, half_ref, held,
+):
+    grid = own_ref.shape[0]
+    one_ref[0:grid, :] = own_ref[...]
+    one_ref[grid:, :] = own_v_ref[...]
+    two_ref[0:grid, :] = other_ref[...]
+    two_ref[grid:, :] = other_v_ref[...]
+    whole_ref[...] = ordered(held, one_ref[...], two_ref[...], bit(0))
     half_rows(whole_ref, half_ref, bit(0))
 
 
@@ -263,20 +281,15 @@
 
 
 def starts_kernel(*refs):
-    others, (prefix_ref, start_ref, sum_ref, later_ref, starts_ref, shifts_ref, held) = refs[:4], refs[4:]
+    others, (prefix_ref, start_ref, starts_ref, shifts_ref, lead_ref, held) = refs[:4], refs[4:]
     chains, grid = prefix_ref.shape[0], prefix_ref.shape[2]
     top = others[3]
     row = lax.broadcasted_iota(jnp.int32, top.shape, 0)
     column = lax.broadcasted_iota(jnp.int32, top.shape, 1)
     held[...] = jnp.where(bit(3) > 0, top[...], jnp.where(row == column, 1.0, 0.0))
-    tail = []
     for level in (2, 1, 0):
         if level == MERGED - 1:
-            for k, part_ref in enumerate((sum_ref, later_ref)):
-                moved = times(held[...], right(part_ref[0:grid, :]))
-                starts_ref[chains + k] = moved[:grid]
-                tail.append(moved[grid : grid + 1] + part_ref[grid : grid + 1, :])
-                tail.append(part_ref[grid + 1 : grid + 2, :])
+            lead_ref[...] = held[...]
 
         @pl.when(bit(level) > 0)
         def _():
@@ -287,16 +300,26 @@
         moved = times(held[...], right(prefix_ref[j - 1]))
         starts_ref[j] = moved[:grid]
         rows.append(moved[grid : grid + 1] + start_ref[j : j + 1, :])
-    shifts_ref[...] = jnp.concatenate([*rows, *tail], axis=0)
-
-
-def send_kernel(end_ref, group_ref, starts_ref, shifts_ref, state_ref, send_ref):
-    chains = starts_ref.shape[0] - 2
+    shifts_ref[...] = jnp.concatenate([*rows, jnp.zeros((VEC - chains, grid), F32)], axis=0)
+
+
+def ahead_kernel(lead_ref, sum_ref, later_ref, ahead_ref, tail_ref):
+    grid = lead_ref.shape[1]
+    tail = []
+    for k, part_ref in enumerate((sum_ref, later_ref)):
+        moved = times(lead_ref[...], right(part_ref[0:grid, :]))
+        ahead_ref[k] = moved[:grid]
+        tail.append(moved[grid : grid + 1] + part_ref[grid : grid + 1, :])
+        tail.append(part_ref[grid + 1 : grid + 2, :])
+    tail_ref[...] = jnp.concatenate([*tail, jnp.zeros((VEC - 4, grid), F32)], axis=0)
+
+
+def send_kernel(end_ref, group_ref, ahead_ref, tail_ref, state_ref, send_ref):
     state = jnp.where(bit(5) > 0, end_ref[...], 0.0)
     state = jnp.where(bit(4) > 0, advance(state, group_ref[...]), state)
     state_ref[...] = state
-    v = times(state, right(starts_ref[chains]))[0:1] + shifts_ref[chains : chains + 1, :]
-    d = shifts_ref[chains + 1 : chains + 2, :]
+    v = times(state, right(ahead_ref[0]))[0:1] + tail_ref[0:1, :]
+    d = tail_ref[1:2, :]
     send_ref[...] = jnp.broadcast_to(jnp.concatenate([d, v], axis=1)[None], send_ref.shape)
 
 
@@ -306,10 +329,10 @@
 
 
 def final_kernel(
-    state_ref, starts_ref, shifts_ref, drive_ref, gains_ref, smooth_ref, transition_ref,
-    filtered_ref, weight_ref, value_ref, found, scan_d, scan_v,
+    state_ref, starts_ref, shifts_ref, ahead_ref, tail_ref, drive_ref, gains_ref, smooth_ref,
+    transition_ref, filtered_ref, weight_ref, value_ref, found, scan_d, scan_v,
 ):
-    chains = starts_ref.shape[0] - 2
+    chains = starts_ref.shape[0]
     frames = drive_ref.shape[0]
     part = lax.axis_index("y")
     step = right(transition_ref[...].T)
@@ -334,8 +357,8 @@
     share = filtered_ref.shape[0]
     mine = pl.ds(pl.multiple_of(part * share, share), share)
     filtered_ref[...] = found[mine, :]
-    later = times(state, right(starts_ref[chains + 1]))[0:1] + shifts_ref[chains + 2 : chains + 3, :]
-    weight_ref[...] = scan_d[mine, :] * shifts_ref[chains + 3 : chains + 4, :]
+    later = times(state, right(ahead_ref[1]))[0:1] + tail_ref[2:3, :]
+    weight_ref[...] = scan_d[mine, :] * tail_ref[3:4, :]
     value_ref[...] = scan_d[mine, :] * later + scan_v[mine, :]
 
 
@@ -378,43 +401,46 @@
     parts = lax.axis_size("y")
     H = pl.BlockSpec(memory_space=pltpu.HBM)
     units = w_in.shape[1]
-    partial = call(
-        network_kernel, [H] * 4, V, shape(frames, grid),
+    matrix, stack = shape(grid, grid), shape(chains, grid, grid)
+    arrays = (features, w_in, b_in[None], output_weight, gains, transition)
+    partial, early = call(
+        network_kernel, [H] * 6, [V, V], [shape(frames, grid), stack],
         [
             pltpu.VMEM(features.shape, BF16), pltpu.VMEM(w_in.shape, BF16),
             pltpu.VMEM((1, units), F32), pltpu.VMEM(output_weight.shape, BF16),
-            pltpu.VMEM((frames, units), F32), pltpu.SemaphoreType.DMA((8 + 3,)),
+            pltpu.VMEM(gains.shape, F32), pltpu.VMEM(transition.shape, F32),
+            pltpu.VMEM((frames, units), F32), pltpu.SemaphoreType.DMA((8 + 5,)),
         ],
-    )(*(pltpu.with_memory_space_constraint(a, pltpu.HBM) for a in (features, w_in, b_in[None], output_weight)))
+    )(*(pltpu.with_memory_space_constraint(a, pltpu.HBM) for a in arrays))
+
+    def moved(a, axis, to):
+        pairs = [(k, to(k)) for k in range(lax.axis_size(axis))]
+        return lax.ppermute(a, axis, [(k, n) for k, n in pairs if n is not None])
+
     partials = [partial] + [
-        lax.ppermute(partial, "y", [(k, (k + s) % parts) for k in range(parts)])
-        for s in range(1, parts)
+        moved(partial, "y", lambda k: (k + s) % parts) for s in range(1, parts)
     ]
-
-    chain, prefix = call(
-        block_kernel, [V, V], [V, V],
-        [shape(chains, grid, grid), shape(chains, grid, grid)],
-    )(gains, transition)
-    whole, drive, start = call(
-        response_kernel, [V] * 9, [V] * 3,
-        [shape(rows, grid), shape(frames, grid), shape(VEC, grid)],
-    )(*partials, final_offset_entries[None], gains, transition, chain, prefix)
+    block, chain, prefix = call(block_kernel, [V] * 3, [V] * 3, [matrix, stack, stack])(
+        gains, transition, early
+    )
+    *partials, block = lax.optimization_barrier((*partials, block))
+    other_block = moved(block, "c", lambda k: 1 - k)
+    ended, drive, start = call(
+        response_kernel, [V] * 8, [V] * 3, [shape(VEC, grid), shape(frames, grid), shape(VEC, grid)],
+    )(*partials, final_offset_entries[None], gains, transition, chain)
+    ended, other_block = lax.optimization_barrier((ended, other_block))
 
     big, small = shape(rows, grid), shape(grid // 2 + VEC, grid)
     held = [pltpu.VMEM((2, rows, grid), F32)]
-
-    def moved(a, axis, to):
-        return lax.ppermute(a, axis, [(k, to(k)) for k in range(lax.axis_size(axis))])
 
     ways = [
         ("c", lambda k: 1 - k), (Z, lambda k: k ^ 1), (Z, lambda k: k ^ 3),
         (Z, lambda k: 7 - k), ("x", lambda k: k ^ 1), ("x", lambda k: 3 - k),
     ]
-    wholes = [whole]
-    others = [moved(whole, *ways[0])]
-    whole, half = call(
-        functools.partial(whole_kernel, 0), [V, V], [V, V], [big, small], held
-    )(whole, others[0])
+    one, two, whole, half = call(
+        core_kernel, [V] * 4, [V] * 4, [big, big, big, small], held
+    )(block, other_block, ended, moved(ended, *ways[0]))
+    wholes, others = [one], [two]
     for level in (1, 2, 3):
         wholes.append(whole)
         mine = moved(half, *ways[level])
@@ -436,6 +462,11 @@
         )(whole, mine, theirs)
         others.append(other)
     mine = moved(half, *ways[4])
+    starts, shifts, lead = call(
+        starts_kernel, [V] * 6, [V] * 3, [stack, shape(VEC, grid), big],
+        [pltpu.VMEM((rows, grid), F32)],
+    )(*others, prefix, start)
+    mine, lead = lax.optimization_barrier((mine, lead))
     if MERGED > 1:
         total, _ = lax.optimization_barrier((total, half))
         total, later = call(
@@ -446,20 +477,19 @@
         functools.partial(end_kernel, 4), [V] * 3, [V, V], [shape(VEC, grid), big], held
     )(whole, mine, theirs)
     end = moved(end, *ways[5])
-    starts, shifts = call(
-        starts_kernel, [V] * 8, [V, V], [shape(chains + 2, grid, grid), shape(VEC, grid)],
-        [pltpu.VMEM((rows, grid), F32)],
-    )(*others, prefix, start, total, later)
+    ahead, tail = call(ahead_kernel, [V] * 3, [V, V], [shape(2, grid, grid), shape(VEC, grid)])(
+        lead, total, later
+    )
 
     share = frames // parts
     state, send = call(
         send_kernel, [V] * 4, [V, V], [shape(VEC, grid), shape(blocks, 1, 2 * grid)]
-    )(end, group, starts, shifts)
+    )(end, group, ahead, tail)
     got = lax.all_to_all(send, among, 0, 0, tiled=True)[:, 0]
     filtered, weight, value = call(
-        final_kernel, [V] * 7, [V] * 3, [shape(share, grid)] * 3,
+        final_kernel, [V] * 9, [V] * 3, [shape(share, grid)] * 3,
         [pltpu.VMEM((frames, grid), F32)] * 3,
-    )(state, starts, shifts, drive, gains, smooth_gains, transition)
+    )(state, starts, shifts, ahead, tail, drive, gains, smooth_gains, transition)
     smoothed = call(smooth_kernel, [V, V, V], V, shape(share, grid))(
         got, weight, value
     )

time: 79.6 us -> 79.8 us (level)
  starting transfers between devices: 31 us -> 32.3 us
    ppermute x15 -> x16, starting transfers between devices: 23.8 us -> 24.7 us  [moved(): return lax.ppermute(a, axis, [(k, n) for k, n in pairs if n is not None])]
    ppermute x15 -> x16, waiting for transfers between devices: 18.8 us -> 18.6 us  [moved(): return lax.ppermute(a, axis, [(k, n) for k, n in pairs if n is not None])]
    pallas_call x6 -> x7, Pallas kernels: 11.7 us -> 11.6 us  [the longest x1 3.89 us: on_device(): call(network_kernel, [H] * 6, [V, V], [shape(frames, grid), stack], [pltp...]
  transfers between devices with their start and end apart: 16 -> 17, of which waited for: 9 -> 10; matrix products, arithmetic and copies ran while one was open for 0% -> 0% of each run, Pallas kernels for 17% -> 17%
where the time goes in v4:
time: 79.8 us; the launch traced here: 78.9 us
  starting transfers between devices  32.3 us (40%)
  waiting for transfers between devices  25.5 us (32%)
  Pallas kernels  20.3 us (25%)
    ppermute x16, starting transfers between devices, moved(): return lax.ppermute(a, axis, [(k, n) for k, n in pairs if n is not None])  24.7 us
    ppermute x16, waiting for transfers between devices, moved(): return lax.ppermute(a, axis, [(k, n) for k, n in pairs if n is not None])  18.6 us
    all_to_all x1, starting transfers between devices, on_device(): got = lax.all_to_all(send, among, 0, 0, tiled=True)[:, 0]  7.58 us
    all_to_all x1, waiting for transfers between devices, on_device(): got = lax.all_to_all(send, among, 0, 0, tiled=True)[:, 0]  6.9 us
    pallas_call x1, Pallas kernels, on_device(): call(summary_kernel, [V] * 6, V, big, [pltpu.VMEM((chains, rows, grid), F...  5.09 us
    pallas_call x1, Pallas kernels, on_device(): call(network_kernel, [H] * 6, [V, V], [shape(frames, grid), stack], [pltp...  3.89 us
    pallas_call x1, Pallas kernels, on_device(): call(block_kernel, [V] * 3, [V] * 3, [matrix, stack, stack])  2.67 us
    pallas_call x1, Pallas kernels, on_device(): call(final_kernel, [V] * 9, [V] * 3, [shape(share, grid)] * 3, [pltpu.VME...  1.96 us
  transfers between devices with their start and end apart: 17, of which 10 were waited for; matrix products, arithmetic and copies ran while one was open for 0% of the time, Pallas kernels for 17%

profile of v4, /device:TPU:1, one launch (start us, length us, event | category | flops | bytes accessed | tf_op | source)
XLA Modules:
  0.0 78.9 jit_solution(17098224756205749354)
XLA Ops:
  0.7 3.9 %shard_map.95 = (f32[32,256]{1,0:T(8,128)S(1)}, f32[4,256,256]{2,1,0:T(8,128)S(1)}) custom-call(bf16[32,2048]{1,0:T(8,128)(2,1)} %features_hbm.1, bf16[2048,1024]{1,0:T(8,128)(2,1)} %w_in_hbm.1, f32[1,1024]{1,0:T(1,128)} %bitcast.7, bf16[1024,256]{1,0:T(8,128)(2,1)} %out_weight_hbm.1, f32[32,256]{1,0:T(8,128)} %gains_ref.7, f32[256,256]{1,0:T(8,128)} %transition_ref.7), custom_call_target="tpu_custom_call" | custom-call | tf_op jit(solution)/shard_map/pallas_call | solution.py:406
  4.6 2.2 %collective-permute-start = (f32[32,256]{1,0:T(8,128)S(1)}, f32[32,256]{1,0:T(8,128)S(1)}, u32[]{:S(2)}, u32[]{:S(2)}) collective-permute-start(f32[32,256]{1,0:T(8,128)S(1)} %get-tuple-element.58.one_ref), channel_id=1, source_target_pairs={{0,1},{1,2},{2,3},{3,0},{4,5},{5,6},{6,7},{7,4},{8,9},{9,10},{10,1... | collective-permute-start | bytes 98312 | tf_op jit(solution)/shard_map/ppermute | solution.py:418
  6.8 2.6 %collective-permute-start.1 = (f32[32,256]{1,0:T(8,128)S(1)}, f32[32,256]{1,0:T(8,128)S(1)}, u32[]{:S(2)}, u32[]{:S(2)}) collective-permute-start(f32[32,256]{1,0:T(8,128)S(1)} %get-tuple-element.58.one_ref), channel_id=1, source_target_pairs={{0,2},{1,3},{2,0},{3,1},{4,6},{5,7},{6,4},{7,5},{8,10},{9,11},{10,... | collective-permute-start | bytes 98312 | tf_op jit(solution)/shard_map/ppermute | solution.py:418
  9.4 1.1 %collective-permute-start.2 = (f32[32,256]{1,0:T(8,128)S(1)}, f32[32,256]{1,0:T(8,128)S(1)}, u32[]{:S(2)}, u32[]{:S(2)}) collective-permute-start(f32[32,256]{1,0:T(8,128)S(1)} %get-tuple-element.58.one_ref), channel_id=1, source_target_pairs={{0,3},{1,0},{2,1},{3,2},{4,7},{5,4},{6,5},{7,6},{8,11},{9,8},{10,9... | collective-permute-start | bytes 98312 | tf_op jit(solution)/shard_map/ppermute | solution.py:418
  10.5 2.7 %shard_map.96 = (f32[256,256]{1,0:T(8,128)S(1)}, f32[4,256,256]{2,1,0:T(8,128)S(1)}, f32[4,256,256]{2,1,0:T(8,128)S(1)}) custom-call(f32[32,256]{1,0:T(8,128)S(1)} %copy-done.1, f32[256,256]{1,0:T(8,128)S(1)} %copy-done, f32[4,256,256]{2,1,0:T(8,128)S(1)} %get-tuple-element.55.early_ref), custom_call_target="tpu_custom_call" | custom-call | tf_op jit(solution)/shard_map/pallas_call | solution.py:423
  13.1 0.0 collective-permute-done.two_ref
  13.2 0.0 collective-permute-done.1.three_ref
  13.2 1.6 %collective-permute-start.3 = (f32[256,256]{1,0:T(8,128)S(1)}, f32[256,256]{1,0:T(8,128)S(1)}, u32[]{:S(2)}, u32[]{:S(2)}) collective-permute-start(f32[256,256]{1,0:T(8,128)S(1)} %get-tuple-element.57.own_ref), channel_id=1, source_target_pairs={{0,4},{4,0},{1,5},{5,1},{2,6},{6,2},{3,7},{7,3},{8,12},{12,8},{9,1... | collective-permute-start | bytes 786440 | tf_op jit(solution)/shard_map/ppermute | solution.py:418
  14.8 1.4 %shard_map.97 = (f32[8,256]{1,0:T(8,128)S(1)}, f32[32,256]{1,0:T(8,128)S(1)}, f32[8,256]{1,0:T(8,128)S(1)}) custom-call(f32[32,256]{1,0:T(8,128)S(1)} %get-tuple-element.58.one_ref, f32[32,256]{1,0:T(8,128)S(1)} %collective-permute-done.two_ref, f32[32,256]{1,0:T(8,128)S(1)} %collective-permute-done.1.three_ref, ...), custom_call_target="tpu_custom_call" | custom-call | tf_op jit(solution)/shard_map/pallas_call | solution.py:428
  16.2 0.0 collective-permute-done.3.other_ref
  16.2 0.1 collective-permute-start.4
  16.3 1.1 %collective-permute-done.4.other_v_ref = f32[8,256]{1,0:T(8,128)S(1)} collective-permute-done((f32[8,256]{1,0:T(8,128)S(1)}, f32[8,256]{1,0:T(8,128)S(1)}, u32[]{:S(2)}, u32[]{:S(2)}) %collective-permute-start.4) | collective-permute-done | bytes 8224 | tf_op jit(solution)/shard_map/ppermute | solution.py:418
  17.4 0.4 shard_map.98
  17.8 1.7 %collective-permute-start.5 = (f32[136,256]{1,0:T(8,128)S(1)}, f32[136,256]{1,0:T(8,128)S(1)}, u32[]{:S(2)}, u32[]{:S(2)}) collective-permute-start(f32[136,256]{1,0:T(8,128)S(1)} %get-tuple-element.67), channel_id=1, source_target_pairs={{0,8},{8,0},{16,24},{24,16},{32,40},{40,32},{48,56},{56,48},{1,9},... | collective-permute-start | bytes 417800 | tf_op jit(solution)/shard_map/ppermute | solution.py:418
  19.6 3.9 %collective-permute-done.5.mine_ref = f32[136,256]{1,0:T(8,128)S(1)} collective-permute-done((f32[136,256]{1,0:T(8,128)S(1)}, f32[136,256]{1,0:T(8,128)S(1)}, u32[]{:S(2)}, u32[]{:S(2)}) %collective-permute-start.5) | collective-permute-done | bytes 139296 | tf_op jit(solution)/shard_map/ppermute | solution.py:418
  23.4 0.8 collective-permute-start.6
  24.2 1.0 %collective-permute-done.6.theirs_ref = f32[136,256]{1,0:T(8,128)S(1)} collective-permute-done((f32[136,256]{1,0:T(8,128)S(1)}, f32[136,256]{1,0:T(8,128)S(1)}, u32[]{:S(2)}, u32[]{:S(2)}) %collective-permute-start.6) | collective-permute-done | bytes 139296 | tf_op jit(solution)/shard_map/ppermute | solution.py:418
  25.2 0.4 shard_map.99
  25.6 4.5 %collective-permute-start.7 = (f32[136,256]{1,0:T(8,128)S(1)}, f32[136,256]{1,0:T(8,128)S(1)}, u32[]{:S(2)}, u32[]{:S(2)}) collective-permute-start(f32[136,256]{1,0:T(8,128)S(1)} %get-tuple-element.69), channel_id=1, source_target_pairs={{0,24},{8,16},{16,8},{24,0},{32,56},{40,48},{48,40},{56,32},{1,25}... | collective-permute-start | bytes 417800 | tf_op jit(solution)/shard_map/ppermute | solution.py:418
  30.0 5.1 %shard_map.100.refs_2_ = f32[264,256]{1,0:T(8,128)S(1)} custom-call(f32[32,256]{1,0:T(8,128)S(1)} %copy-done.1, f32[32,256]{1,0:T(8,128)S(1)} %copy-done.2, f32[256,256]{1,0:T(8,128)S(1)} %copy-done, f32[32,256]{1,0:T(8,128)S(1)} %get-tuple-element.71.drive_ref, f32[4,256,256]{2,1,0:T(8,128)S(1)} %get-tuple-element.72.prefix_ref.refs_4_, ...), custom_call_target="tpu_custom_call" | custom-call | tf_op jit(solution)/shard_map/pallas_call | solution.py:449
  35.1 0.0 collective-permute-done.7.mine_ref
  35.1 0.7 collective-permute-start.8
  35.9 0.1 collective-permute-start.10
  36.0 0.9 %collective-permute-done.8.theirs_ref = f32[136,256]{1,0:T(8,128)S(1)} collective-permute-done((f32[136,256]{1,0:T(8,128)S(1)}, f32[136,256]{1,0:T(8,128)S(1)}, u32[]{:S(2)}, u32[]{:S(2)}) %collective-permute-start.8) | collective-permute-done | bytes 139296 | tf_op jit(solution)/shard_map/ppermute | solution.py:418
  36.9 0.4 shard_map.101
  37.3 3.5 %collective-permute-start.9 = (f32[136,256]{1,0:T(8,128)S(1)}, f32[136,256]{1,0:T(8,128)S(1)}, u32[]{:S(2)}, u32[]{:S(2)}) collective-permute-start(f32[136,256]{1,0:T(8,128)S(1)} %get-tuple-element.76), channel_id=1, source_target_pairs={{0,56},{8,48},{16,40},{24,32},{32,24},{40,16},{48,8},{56,0},{1,57}... | collective-permute-start | bytes 417800 | tf_op jit(solution)/shard_map/ppermute | solution.py:418
  40.7 0.3 shard_map.102
  41.0 6.5 %collective-permute-done.9.mine_ref = f32[136,256]{1,0:T(8,128)S(1)} collective-permute-done((f32[136,256]{1,0:T(8,128)S(1)}, f32[136,256]{1,0:T(8,128)S(1)}, u32[]{:S(2)}, u32[]{:S(2)}) %collective-permute-start.9) | collective-permute-done | bytes 139296 | tf_op jit(solution)/shard_map/ppermute | solution.py:418
  47.5 0.9 %collective-permute-start.11 = (f32[136,256]{1,0:T(8,128)S(1)}, f32[136,256]{1,0:T(8,128)S(1)}, u32[]{:S(2)}, u32[]{:S(2)}) collective-permute-start(f32[136,256]{1,0:T(8,128)S(1)} %collective-permute-done.9.mine_ref), channel_id=1, source_target_pairs={{0,4},{4,0},{1,5},{5,1},{2,6},{6,2},{3,7},{7,3},{8,12},{12,8},{9,1... | collective-permute-start | bytes 417800 | tf_op jit(solution)/shard_map/ppermute | solution.py:418
  48.4 1.0 %collective-permute-done.11.theirs_ref = f32[136,256]{1,0:T(8,128)S(1)} collective-permute-done((f32[136,256]{1,0:T(8,128)S(1)}, f32[136,256]{1,0:T(8,128)S(1)}, u32[]{:S(2)}, u32[]{:S(2)}) %collective-permute-start.11) | collective-permute-done | bytes 139296 | tf_op jit(solution)/shard_map/ppermute | solution.py:418
  49.3 0.4 shard_map.103
  49.8 1.3 %collective-permute-start.12 = (f32[136,256]{1,0:T(8,128)S(1)}, f32[136,256]{1,0:T(8,128)S(1)}, u32[]{:S(2)}, u32[]{:S(2)}) collective-permute-start(f32[136,256]{1,0:T(8,128)S(1)} %get-tuple-element.83), channel_id=1, source_target_pairs={{0,64},{64,0},{128,192},{192,128},{1,65},{65,1},{129,193},{193,129... | collective-permute-start | bytes 417800 | tf_op jit(solution)/shard_map/ppermute | solution.py:418
  51.1 0.0 collective-permute-start.15
  51.1 0.9 %shard_map.104 = (f32[4,256,256]{2,1,0:T(8,128)S(1)}, f32[8,256]{1,0:T(8,128)S(1)}, f32[264,256]{1,0:T(8,128)S(1)}) custom-call(f32[264,256]{1,0:T(8,128)S(1)} %get-tuple-element.78.refs_1_.refs_0_, f32[264,256]{1,0:T(8,128)S(1)} %get-tuple-element.84.refs_1_, f32[264,256]{1,0:T(8,128)S(1)} %get-tuple-element.85.refs_2_, ...), custom_call_target="tpu_custom_call" | custom-call | tf_op jit(solution)/shard_map/pallas_call | solution.py:465
  51.9 2.8 %collective-permute-done.12.mine_ref = f32[136,256]{1,0:T(8,128)S(1)} collective-permute-done((f32[136,256]{1,0:T(8,128)S(1)}, f32[136,256]{1,0:T(8,128)S(1)}, u32[]{:S(2)}, u32[]{:S(2)}) %collective-permute-start.12) | collective-permute-done | bytes 139296 | tf_op jit(solution)/shard_map/ppermute | solution.py:418
  54.7 1.2 %collective-permute-start.13 = (f32[136,256]{1,0:T(8,128)S(1)}, f32[136,256]{1,0:T(8,128)S(1)}, u32[]{:S(2)}, u32[]{:S(2)}) collective-permute-start(f32[136,256]{1,0:T(8,128)S(1)} %collective-permute-done.12.mine_ref), channel_id=1, source_target_pairs={{0,4},{4,0},{1,5},{5,1},{2,6},{6,2},{3,7},{7,3},{8,12},{12,8},{9,1... | collective-permute-start | bytes 417800 | tf_op jit(solution)/shard_map/ppermute | solution.py:418
  55.9 1.0 %collective-permute-done.13.theirs_ref = f32[136,256]{1,0:T(8,128)S(1)} collective-permute-done((f32[136,256]{1,0:T(8,128)S(1)}, f32[136,256]{1,0:T(8,128)S(1)}, u32[]{:S(2)}, u32[]{:S(2)}) %collective-permute-start.13) | collective-permute-done | bytes 139296 | tf_op jit(solution)/shard_map/ppermute | solution.py:418
  56.9 0.3 shard_map.105
  57.2 2.5 %collective-permute-start.14 = (f32[8,256]{1,0:T(8,128)S(1)}, f32[8,256]{1,0:T(8,128)S(1)}, u32[]{:S(2)}, u32[]{:S(2)}) collective-permute-start(f32[8,256]{1,0:T(8,128)S(1)} %get-tuple-element.89), channel_id=1, source_target_pairs={{0,192},{64,128},{128,64},{192,0},{1,193},{65,129},{129,65},{193,1... | collective-permute-start | bytes 24584 | tf_op jit(solution)/shard_map/ppermute | solution.py:418
  59.7 0.0 collective-permute-done.15.refs_3_
  59.7 0.3 shard_map.106
  60.0 0.4 shard_map.107
  60.4 0.5 collective-permute-done.14.end_ref
  60.9 0.9 %shard_map.108 = (f32[8,256]{1,0:T(8,128)S(1)}, f32[16,1,512]{2,1,0:T(1,128)}) custom-call(f32[8,256]{1,0:T(8,128)S(1)} %collective-permute-done.14.end_ref, f32[264,256]{1,0:T(8,128)S(1)} %get-tuple-element.90.group_ref, f32[2,256,256]{2,1,0:T(8,128)S(1)} %get-tuple-element.97.ahead_ref, f32[8,256]{1,0:T(8,128)S(1)} %get-tuple-element.98.tail_ref), custom_call_target="tpu_custom_call" | custom-call | tf_op jit(solution)/shard_map/pallas_call | solution.py:485
  61.8 7.6 %all-to-all-start = ((f32[16,1,512]{2,1,0:T(1,128)}), f32[16,1,512]{2,1,0:T(1,128)S(1)}, u32[]{:S(2)}, u32[]{:S(2)}) async-start(f32[16,1,512]{2,1,0:T(1,128)} %get-tuple-element.103), calls=%async_computation | async-start | bytes 65536 | tf_op jit(solution)/shard_map/all_to_all | solution.py:488
  69.4 2.0 %shard_map.109 = (f32[8,256]{1,0:T(8,128)}, f32[8,256]{1,0:T(8,128)S(1)}, f32[8,256]{1,0:T(8,128)S(1)}) custom-call(f32[8,256]{1,0:T(8,128)S(1)} %get-tuple-element.99.state_ref, f32[4,256,256]{2,1,0:T(8,128)S(1)} %get-tuple-element.100.starts_ref, f32[8,256]{1,0:T(8,128)S(1)} %get-tuple-element.101.shifts_ref, ...), custom_call_target="tpu_custom_call" | custom-call | tf_op jit(solution)/shard_map/pallas_call | solution.py:489
  71.3 6.9 %all-to-all-done = f32[16,1,512]{2,1,0:T(1,128)S(1)} async-done(((f32[16,1,512]{2,1,0:T(1,128)}), f32[16,1,512]{2,1,0:T(1,128)S(1)}, u32[]{:S(2)}, u32[]{:S(2)}) %all-to-all-start) | async-done | bytes 32800 | tf_op jit(solution)/shard_map/all_to_all | solution.py:488
  78.2 0.7 shard_map.110
  (11 shorter events, 0.0 us)
Async XLA Ops:
  0.6 9.8 %copy-start = (f32[256,256]{1,0:T(8,128)S(1)}, f32[256,256]{1,0:T(8,128)}, u32[]{:S(2)}) copy-start(f32[256,256]{1,0:T(8,128)} %transition_ref.7) | copy-start | bytes 786436
  0.6 9.8 %copy-start.1 = (f32[32,256]{1,0:T(8,128)S(1)}, f32[32,256]{1,0:T(8,128)}, u32[]{:S(2)}) copy-start(f32[32,256]{1,0:T(8,128)} %gains_ref.7) | copy-start | bytes 98308
  0.7 14.1 %copy-start.3 = (f32[256]{0:T(256)S(1)}, f32[256]{0:T(256)}, u32[]{:S(2)}) copy-start(f32[256]{0:T(256)} %param.12) | copy-start | bytes 3076
  0.7 29.4 %copy-start.2 = (f32[32,256]{1,0:T(8,128)S(1)}, f32[32,256]{1,0:T(8,128)}, u32[]{:S(2)}) copy-start(f32[32,256]{1,0:T(8,128)} %smooth_ref.3) | copy-start | bytes 98308
  4.6 8.6 %collective-permute-start = (f32[32,256]{1,0:T(8,128)S(1)}, f32[32,256]{1,0:T(8,128)S(1)}, u32[]{:S(2)}, u32[]{:S(2)}) collective-permute-start(f32[32,256]{1,0:T(8,128)S(1)} %get-tuple-element.58.one_ref), channel_id=1, source_target_pairs={{0,1},{1,2},{2,3},{3,0},{4,5},{5,6},{6,7},{7,4},{8,9},{9,10},{10,1... | collective-permute-start | bytes 98312 | tf_op jit(solution)/shard_map/ppermute | solution.py:418
  6.8 6.4 %collective-permute-start.1 = (f32[32,256]{1,0:T(8,128)S(1)}, f32[32,256]{1,0:T(8,128)S(1)}, u32[]{:S(2)}, u32[]{:S(2)}) collective-permute-start(f32[32,256]{1,0:T(8,128)S(1)} %get-tuple-element.58.one_ref), channel_id=1, source_target_pairs={{0,2},{1,3},{2,0},{3,1},{4,6},{5,7},{6,4},{7,5},{8,10},{9,11},{10,... | collective-permute-start | bytes 98312 | tf_op jit(solution)/shard_map/ppermute | solution.py:418
  9.4 3.8 %collective-permute-start.2 = (f32[32,256]{1,0:T(8,128)S(1)}, f32[32,256]{1,0:T(8,128)S(1)}, u32[]{:S(2)}, u32[]{:S(2)}) collective-permute-start(f32[32,256]{1,0:T(8,128)S(1)} %get-tuple-element.58.one_ref), channel_id=1, source_target_pairs={{0,3},{1,0},{2,1},{3,2},{4,7},{5,4},{6,5},{7,6},{8,11},{9,8},{10,9... | collective-permute-start | bytes 98312 | tf_op jit(solution)/shard_map/ppermute | solution.py:418
  13.2 3.0 %collective-permute-start.3 = (f32[256,256]{1,0:T(8,128)S(1)}, f32[256,256]{1,0:T(8,128)S(1)}, u32[]{:S(2)}, u32[]{:S(2)}) collective-permute-start(f32[256,256]{1,0:T(8,128)S(1)} %get-tuple-element.57.own_ref), channel_id=1, source_target_pairs={{0,4},{4,0},{1,5},{5,1},{2,6},{6,2},{3,7},{7,3},{8,12},{12,8},{9,1... | collective-permute-start | bytes 786440 | tf_op jit(solution)/shard_map/ppermute | solution.py:418
  16.2 1.3 %collective-permute-start.4 = (f32[8,256]{1,0:T(8,128)S(1)}, f32[8,256]{1,0:T(8,128)S(1)}, u32[]{:S(2)}, u32[]{:S(2)}) collective-permute-start(f32[8,256]{1,0:T(8,128)S(1)} %get-tuple-element.65.own_v_ref), channel_id=1, source_target_pairs={{0,4},{4,0},{1,5},{5,1},{2,6},{6,2},{3,7},{7,3},{8,12},{12,8},{9,1... | collective-permute-start | bytes 24584 | tf_op jit(solution)/shard_map/ppermute | solution.py:418
  17.8 5.6 %collective-permute-start.5 = (f32[136,256]{1,0:T(8,128)S(1)}, f32[136,256]{1,0:T(8,128)S(1)}, u32[]{:S(2)}, u32[]{:S(2)}) collective-permute-start(f32[136,256]{1,0:T(8,128)S(1)} %get-tuple-element.67), channel_id=1, source_target_pairs={{0,8},{8,0},{16,24},{24,16},{32,40},{40,32},{48,56},{56,48},{1,9},... | collective-permute-start | bytes 417800 | tf_op jit(solution)/shard_map/ppermute | solution.py:418
  23.4 1.8 %collective-permute-start.6 = (f32[136,256]{1,0:T(8,128)S(1)}, f32[136,256]{1,0:T(8,128)S(1)}, u32[]{:S(2)}, u32[]{:S(2)}) collective-permute-start(f32[136,256]{1,0:T(8,128)S(1)} %collective-permute-done.5.mine_ref), channel_id=1, source_target_pairs={{0,4},{4,0},{1,5},{5,1},{2,6},{6,2},{3,7},{7,3},{8,12},{12,8},{9,1... | collective-permute-start | bytes 417800 | tf_op jit(solution)/shard_map/ppermute | solution.py:418
  25.6 9.6 %collective-permute-start.7 = (f32[136,256]{1,0:T(8,128)S(1)}, f32[136,256]{1,0:T(8,128)S(1)}, u32[]{:S(2)}, u32[]{:S(2)}) collective-permute-start(f32[136,256]{1,0:T(8,128)S(1)} %get-tuple-element.69), channel_id=1, source_target_pairs={{0,24},{8,16},{16,8},{24,0},{32,56},{40,48},{48,40},{56,32},{1,25}... | collective-permute-start | bytes 417800 | tf_op jit(solution)/shard_map/ppermute | solution.py:418
  35.1 1.7 %collective-permute-start.8 = (f32[136,256]{1,0:T(8,128)S(1)}, f32[136,256]{1,0:T(8,128)S(1)}, u32[]{:S(2)}, u32[]{:S(2)}) collective-permute-start(f32[136,256]{1,0:T(8,128)S(1)} %collective-permute-done.7.mine_ref), channel_id=1, source_target_pairs={{0,4},{4,0},{1,5},{5,1},{2,6},{6,2},{3,7},{7,3},{8,12},{12,8},{9,1... | collective-permute-start | bytes 417800 | tf_op jit(solution)/shard_map/ppermute | solution.py:418
  35.9 4.9 %collective-permute-start.10 = (f32[264,256]{1,0:T(8,128)S(1)}, f32[264,256]{1,0:T(8,128)S(1)}, u32[]{:S(2)}, u32[]{:S(2)}) collective-permute-start(f32[264,256]{1,0:T(8,128)S(1)} %shard_map.100.refs_2_), channel_id=1, source_target_pairs={{0,4},{4,0},{1,5},{5,1},{2,6},{6,2},{3,7},{7,3},{8,12},{12,8},{9,1... | collective-permute-start | bytes 811016 | tf_op jit(solution)/shard_map/ppermute | solution.py:418
  37.3 10.2 %collective-permute-start.9 = (f32[136,256]{1,0:T(8,128)S(1)}, f32[136,256]{1,0:T(8,128)S(1)}, u32[]{:S(2)}, u32[]{:S(2)}) collective-permute-start(f32[136,256]{1,0:T(8,128)S(1)} %get-tuple-element.76), channel_id=1, source_target_pairs={{0,56},{8,48},{16,40},{24,32},{32,24},{40,16},{48,8},{56,0},{1,57}... | collective-permute-start | bytes 417800 | tf_op jit(solution)/shard_map/ppermute | solution.py:418
  47.5 1.9 %collective-permute-start.11 = (f32[136,256]{1,0:T(8,128)S(1)}, f32[136,256]{1,0:T(8,128)S(1)}, u32[]{:S(2)}, u32[]{:S(2)}) collective-permute-start(f32[136,256]{1,0:T(8,128)S(1)} %collective-permute-done.9.mine_ref), channel_id=1, source_target_pairs={{0,4},{4,0},{1,5},{5,1},{2,6},{6,2},{3,7},{7,3},{8,12},{12,8},{9,1... | collective-permute-start | bytes 417800 | tf_op jit(solution)/shard_map/ppermute | solution.py:418
  49.8 5.0 %collective-permute-start.12 = (f32[136,256]{1,0:T(8,128)S(1)}, f32[136,256]{1,0:T(8,128)S(1)}, u32[]{:S(2)}, u32[]{:S(2)}) collective-permute-start(f32[136,256]{1,0:T(8,128)S(1)} %get-tuple-element.83), channel_id=1, source_target_pairs={{0,64},{64,0},{128,192},{192,128},{1,65},{65,1},{129,193},{193,129... | collective-permute-start | bytes 417800 | tf_op jit(solution)/shard_map/ppermute | solution.py:418
  51.1 8.6 %collective-permute-start.15 = (f32[264,256]{1,0:T(8,128)S(1)}, f32[264,256]{1,0:T(8,128)S(1)}, u32[]{:S(2)}, u32[]{:S(2)}) collective-permute-start(f32[264,256]{1,0:T(8,128)S(1)} %get-tuple-element.93.refs_2_), channel_id=1, source_target_pairs={{0,8},{8,0},{16,24},{24,16},{32,40},{40,32},{48,56},{56,48},{1,9},... | collective-permute-start | bytes 811016 | tf_op jit(solution)/shard_map/ppermute | solution.py:418
  54.7 2.2 %collective-permute-start.13 = (f32[136,256]{1,0:T(8,128)S(1)}, f32[136,256]{1,0:T(8,128)S(1)}, u32[]{:S(2)}, u32[]{:S(2)}) collective-permute-start(f32[136,256]{1,0:T(8,128)S(1)} %collective-permute-done.12.mine_ref), channel_id=1, source_target_pairs={{0,4},{4,0},{1,5},{5,1},{2,6},{6,2},{3,7},{7,3},{8,12},{12,8},{9,1... | collective-permute-start | bytes 417800 | tf_op jit(solution)/shard_map/ppermute | solution.py:418
  57.2 3.7 %collective-permute-start.14 = (f32[8,256]{1,0:T(8,128)S(1)}, f32[8,256]{1,0:T(8,128)S(1)}, u32[]{:S(2)}, u32[]{:S(2)}) collective-permute-start(f32[8,256]{1,0:T(8,128)S(1)} %get-tuple-element.89), channel_id=1, source_target_pairs={{0,192},{64,128},{128,64},{192,0},{1,193},{65,129},{129,65},{193,1... | collective-permute-start | bytes 24584 | tf_op jit(solution)/shard_map/ppermute | solution.py:418
  61.8 16.4 %all-to-all-start = ((f32[16,1,512]{2,1,0:T(1,128)}), f32[16,1,512]{2,1,0:T(1,128)S(1)}, u32[]{:S(2)}, u32[]{:S(2)}) async-start(f32[16,1,512]{2,1,0:T(1,128)} %get-tuple-element.103), calls=%async_computation | async-start | bytes 65536 | tf_op jit(solution)/shard_map/all_to_all | solution.py:488
